TPU v7x, 32 devices: a whole 2x2x4 slice. The times are simulated.
32 devices in a mesh: shard: 4 (over z), context: 2 (over y), tensor: 4 (over x, core).
Axes of the slice: x: 2, y: 2, z: 4, core: 2. Of those that a mesh axis runs over, the one named last changes fastest.
Arguments:
- hidden_in: bfloat16 [4, 1024, 2048], P('shard', 'context'), may hold values from -6 to 6
- cotangent: bfloat16 [4, 1024, 2048], P('shard', 'context'), may hold values from -6 to 6
- segment_ids: int32 [4, 1024], P('shard'), may hold values from 0 to 10, as said below
- positions: int32 [4, 1024], P('shard', 'context'), may hold values from 0 to 999, as said below
- attention_gain: bfloat16 [2048], P('shard'), may hold values from 0.5 to 1.5
- query_weight: bfloat16 [2048, 2048], P('shard', 'tensor'), may hold values from -0.125 to 0.125
- key_weight: bfloat16 [2048, 512], P('shard', 'tensor'), may hold values from -0.125 to 0.125
- value_weight: bfloat16 [2048, 512], P('shard', 'tensor'), may hold values from -0.125 to 0.125
- output_weight: bfloat16 [2048, 2048], P('tensor', 'shard'), may hold values from -0.75 to 0.75
- feed_gain: bfloat16 [2048], P('shard'), may hold values from 0.5 to 1.5
- gate_weight: bfloat16 [2048, 8192], P('shard', 'tensor'), may hold values from -0.125 to 0.125
- up_weight: bfloat16 [2048, 8192], P('shard', 'tensor'), may hold values from -0.125 to 0.125
- down_weight: bfloat16 [8192, 2048], P('tensor', 'shard'), may hold values from -0.0625 to 0.0625
Outputs:
- layer_out: bfloat16 [4, 1024, 2048], P('shard', ('context', 'tensor'))
- grad_input: float32 [4, 1024, 2048], P('shard', ('context', 'tensor'))
- grad_attention_gain: float32 [2048], P('shard')
- grad_query: float32 [2048, 2048], P('shard', 'tensor')
- grad_key: float32 [2048, 512], P('shard', 'tensor')
- grad_value: float32 [2048, 512], P('shard', 'tensor')
- grad_output: float32 [2048, 2048], P('tensor', 'shard')
- grad_feed_gain: float32 [2048], P('shard')
- grad_gate: float32 [2048, 8192], P('shard', 'tensor')
- grad_up: float32 [2048, 8192], P('shard', 'tensor')
- grad_down: float32 [8192, 2048], P('tensor', 'shard')
Inputs may be any that keep to these rules, and one draw needn't show every extreme that they name: `segment_ids`: segment ids count the documents of a sequence from 0 in order; every document holds 100 to 1000 tokens (rounded down, at least 1), except the last of a sequence, which may be shorter. `positions`: positions count the tokens of each document from 0 at its first token.
All inputs are finite; a program needn't handle non-finite values.
Results may differ from a plain program's by a relative error of at most 0.018.
Values may be sent and summed in bfloat16 or wider, within the bound.
No kernel may reach another device: no remote copies, remote signals or barrier semaphores. Data moves between devices by JAX's collectives and lax.ppermute only.
A program may use at most 256 MiB of HBM per device.

v0:
```python
import math

import jax
import jax.numpy as jnp
from jax import lax
from jax.sharding import PartitionSpec as P

HEAD = 64


NORM_EPS = 1e-05
ROPE_BASE = 500000.0
MASKED = -1e30


def contract(left, right, left_dim, right_dim):
    return lax.dot_general(
        left, right, (((left_dim,), (right_dim,)), ((), ())), preferred_element_type=jnp.float32
    )


def rms_forward(values, gain):
    inverse = lax.rsqrt(jnp.mean(values * values, axis=-1, keepdims=True) + NORM_EPS)
    normed = values * inverse
    return (normed * gain.astype(jnp.float32), normed, inverse)


def rms_backward(upstream, normed, inverse, gain):
    scaled = upstream * gain.astype(jnp.float32)
    result = inverse * (scaled - normed * jnp.mean(scaled * normed, axis=-1, keepdims=True))
    return (result, jnp.sum(upstream * normed, axis=(0, 1)))


def rope_angles(positions):
    inverse_freq = ROPE_BASE ** (-(jnp.arange(HEAD // 2, dtype=jnp.float32) * 2.0 / HEAD))
    angles = positions.astype(jnp.float32)[:, None] * inverse_freq[None, :]
    return (jnp.cos(angles)[:, None, :], jnp.sin(angles)[:, None, :])


def rotate(tensor, cosine, sine_part, turn):
    first = tensor[..., : HEAD // 2]
    second = tensor[..., HEAD // 2 :]
    return jnp.concatenate(
        [first * cosine - turn * second * sine_part, second * cosine + turn * first * sine_part],
        axis=-1,
    )


def visible(segment_row, row_start, block_rows):
    length = segment_row.shape[0]
    query_index = row_start + jnp.arange(block_rows, dtype=jnp.int32)
    key_index = jnp.arange(length, dtype=jnp.int32)
    query_segment = lax.dynamic_slice_in_dim(segment_row, row_start, block_rows)
    return (query_index[:, None] >= key_index[None, :]) & (
        query_segment[:, None] == segment_row[None, :]
    )


def head_scores(query_block, key_block, allowed, scale):
    scores = (
        jnp.einsum("qgd,td->gqt", query_block, key_block, preferred_element_type=jnp.float32)
        * scale
    )
    return jnp.where(allowed[None], scores, MASKED)


def full_total(partial_value):
    return lax.psum(partial_value, "tensor")


def own_rows(values, share_count):
    return lax.dynamic_slice_in_dim(values, lax.axis_index("tensor") * share_count, share_count, 1)


def reduce_grads(terms):
    shares = (
        lax.psum_scatter(
            terms[0].astype(jnp.bfloat16), "shard", scatter_dimension=0, tiled=True
        ).astype(jnp.float32),
        lax.psum_scatter(
            terms[1].astype(jnp.bfloat16), "shard", scatter_dimension=0, tiled=True
        ).astype(jnp.float32),
        lax.psum_scatter(
            terms[2].astype(jnp.bfloat16), "shard", scatter_dimension=0, tiled=True
        ).astype(jnp.float32),
        lax.psum_scatter(
            terms[3].astype(jnp.bfloat16), "shard", scatter_dimension=1, tiled=True
        ).astype(jnp.float32),
    )
    return (
        lax.psum(shares[0].astype(jnp.bfloat16), "context").astype(jnp.float32),
        lax.psum(shares[1].astype(jnp.bfloat16), "context").astype(jnp.float32),
        lax.psum(shares[2].astype(jnp.bfloat16), "context").astype(jnp.float32),
        lax.psum(shares[3].astype(jnp.bfloat16), "context").astype(jnp.float32),
    )


def local(
    hidden_in,
    cotangent,
    segment_ids,
    positions,
    attention_gain,
    query_weight,
    key_weight,
    value_weight,
    output_weight,
    feed_gain,
    gate_weight,
    up_weight,
    down_weight,
):
    seq_count, local_rows, model_width = hidden_in.shape
    row_count = seq_count * local_rows
    share_count = local_rows // lax.axis_size("tensor")
    scale = 1.0 / math.sqrt(HEAD)
    gathered = (
        lax.all_gather(attention_gain, "shard", axis=0, tiled=True),
        lax.all_gather(query_weight, "shard", axis=0, tiled=True),
        lax.all_gather(key_weight, "shard", axis=0, tiled=True),
        lax.all_gather(value_weight, "shard", axis=0, tiled=True),
        lax.all_gather(output_weight, "shard", axis=1, tiled=True),
        lax.all_gather(feed_gain, "shard", axis=0, tiled=True),
        lax.all_gather(gate_weight, "shard", axis=0, tiled=True),
        lax.all_gather(up_weight, "shard", axis=0, tiled=True),
        lax.all_gather(down_weight, "shard", axis=1, tiled=True),
    )
    (
        gain_one,
        query_full,
        key_full,
        value_full,
        output_full,
        gain_two,
        gate_full,
        up_full,
        down_full,
    ) = gathered
    heads_dev = query_full.shape[1] // HEAD
    kv_dev = key_full.shape[1] // HEAD
    group_size = heads_dev // kv_dev
    group_cols = group_size * HEAD
    block_rows = min(512, local_rows)
    offset = lax.axis_index("context") * local_rows
    input_wide = hidden_in.astype(jnp.float32)
    normed_one, unit_one, inverse_one = rms_forward(input_wide, gain_one)
    normed_one_b = normed_one.astype(jnp.bfloat16).reshape(row_count, model_width)
    cosine, sine_part = rope_angles(positions.reshape(row_count))
    query_rot = rotate(
        contract(normed_one_b, query_full, 1, 0).reshape(row_count, heads_dev, HEAD),
        cosine,
        sine_part,
        1.0,
    )
    query_b = query_rot.astype(jnp.bfloat16).reshape(seq_count, local_rows, heads_dev * HEAD)
    key_rot = rotate(
        contract(normed_one_b, key_full, 1, 0).reshape(row_count, kv_dev, HEAD),
        cosine,
        sine_part,
        1.0,
    )
    key_b = key_rot.astype(jnp.bfloat16).reshape(seq_count, local_rows, kv_dev * HEAD)
    value_b = (
        contract(normed_one_b, value_full, 1, 0)
        .astype(jnp.bfloat16)
        .reshape(seq_count, local_rows, kv_dev * HEAD)
    )
    key_all, value_all = (
        lax.all_gather(key_b, "context", axis=1, tiled=True),
        lax.all_gather(value_b, "context", axis=1, tiled=True),
    )
    seq_index = 0
    head_outputs = []
    head_totals = []
    for head_index in range(kv_dev):
        key_block = key_all[seq_index, :, head_index * HEAD : (head_index + 1) * HEAD]
        value_block = value_all[seq_index, :, head_index * HEAD : (head_index + 1) * HEAD]
        row_start = 0
        query_block = query_b[
            seq_index,
            row_start : row_start + block_rows,
            head_index * group_cols : (head_index + 1) * group_cols,
        ].reshape(block_rows, group_size, HEAD)
        allowed = visible(segment_ids[seq_index], offset + row_start, block_rows)
        scores = head_scores(query_block, key_block, allowed, scale)
        log_total = jnp.log(jnp.sum(jnp.exp(scores), axis=-1, keepdims=True))
        weights_b = jnp.exp(scores - log_total).astype(jnp.bfloat16)
        attended = jnp.einsum(
            "gqt,td->qgd", weights_b, value_block, preferred_element_type=jnp.float32
        ).astype(jnp.bfloat16)
        block_outputs = attended.reshape(block_rows, group_cols)
        block_totals = [log_total]
        head_outputs.append(block_outputs)
        head_totals.append(block_totals)
    attended_rows = jnp.concatenate(head_outputs, axis=1)
    saved_totals = [head_totals]
    attention_part = contract(attended_rows, output_full, 1, 0).reshape(
        seq_count, local_rows, model_width
    )
    residual = input_wide + full_total(attention_part)
    normed_two, unit_two, inverse_two = rms_forward(residual, gain_two)
    normed_two_b = normed_two.astype(jnp.bfloat16)
    normed_two_flat = normed_two_b.reshape(row_count, model_width)
    gate_pre = contract(normed_two_flat, gate_full, 1, 0)
    up_pre = contract(normed_two_flat, up_full, 1, 0)
    sigmoid_gate = jax.nn.sigmoid(gate_pre)
    hidden_b = (gate_pre * sigmoid_gate * up_pre).astype(jnp.bfloat16)
    feed_part = contract(hidden_b, down_full, 1, 0).reshape(seq_count, local_rows, model_width)
    layer_out = own_rows(residual + full_total(feed_part), share_count).astype(jnp.bfloat16)
    gathered = (
        lax.all_gather(attention_gain, "shard", axis=0, tiled=True),
        lax.all_gather(query_weight, "shard", axis=0, tiled=True),
        lax.all_gather(key_weight, "shard", axis=0, tiled=True),
        lax.all_gather(value_weight, "shard", axis=0, tiled=True),
        lax.all_gather(output_weight, "shard", axis=1, tiled=True),
        lax.all_gather(feed_gain, "shard", axis=0, tiled=True),
        lax.all_gather(gate_weight, "shard", axis=0, tiled=True),
        lax.all_gather(up_weight, "shard", axis=0, tiled=True),
        lax.all_gather(down_weight, "shard", axis=1, tiled=True),
    )
    (
        gain_one,
        query_full,
        key_full,
        value_full,
        output_full,
        gain_two,
        gate_full,
        up_full,
        down_full,
    ) = gathered
    cot_b = cotangent.reshape(row_count, model_width)
    cot_wide = cotangent.astype(jnp.float32)
    grad_hidden = contract(cot_b, down_full, 1, 1)
    grad_gate_pre = (
        grad_hidden * up_pre * sigmoid_gate * (1.0 + gate_pre * (1.0 - sigmoid_gate))
    ).astype(jnp.bfloat16)
    grad_up_pre = (grad_hidden * gate_pre * sigmoid_gate).astype(jnp.bfloat16)
    grad_down = contract(hidden_b, cot_b, 0, 0)
    grad_gate = contract(normed_two_flat, grad_gate_pre, 0, 0)
    grad_up = contract(normed_two_flat, grad_up_pre, 0, 0)
    feed_back = (
        contract(grad_gate_pre, gate_full, 1, 1) + contract(grad_up_pre, up_full, 1, 1)
    ).reshape(seq_count, local_rows, model_width)
    grad_normed_two = full_total(feed_back)
    back_two, gain_two_term = rms_backward(grad_normed_two, unit_two, inverse_two, gain_two)
    grad_residual = cot_wide + back_two
    grad_residual_b = grad_residual.astype(jnp.bfloat16)
    feed_terms = (gain_two_term, grad_gate, grad_up, grad_down)
    grad_residual_flat = grad_residual_b.reshape(row_count, model_width)
    grad_output = contract(attended_rows, grad_residual_flat, 0, 0)
    grad_attended = contract(grad_residual_flat, output_full, 1, 1).astype(jnp.bfloat16)
    seq_index = 0
    head_query = []
    head_key = []
    head_value = []
    for head_index in range(kv_dev):
        key_block = key_all[seq_index, :, head_index * HEAD : (head_index + 1) * HEAD]
        value_block = value_all[seq_index, :, head_index * HEAD : (head_index + 1) * HEAD]
        key_sum = jnp.zeros(key_block.shape, jnp.float32)
        value_sum = jnp.zeros(value_block.shape, jnp.float32)
        block_query = []
        for block_index, row_start in enumerate(range(0, local_rows, block_rows)):
            column_low = head_index * group_cols
            row_low = seq_index * local_rows + row_start
            query_block = query_b[
                seq_index, row_start : row_start + block_rows, column_low : column_low + group_cols
            ].reshape(block_rows, group_size, HEAD)
            out_block = attended_rows[
                row_low : row_low + block_rows, column_low : column_low + group_cols
            ].reshape(block_rows, group_size, HEAD)
            upstream = grad_attended[
                row_low : row_low + block_rows, column_low : column_low + group_cols
            ].reshape(block_rows, group_size, HEAD)
            allowed = visible(segment_ids[seq_index], offset + row_start, block_rows)
            scores = head_scores(query_block, key_block, allowed, scale)
            probability = jnp.exp(scores - saved_totals[seq_index][head_index][block_index])
            weights_b = probability.astype(jnp.bfloat16)
            grad_probs = jnp.einsum(
                "qgd,td->gqt", upstream, value_block, preferred_element_type=jnp.float32
            )
            row_dot = jnp.transpose(
                jnp.sum(upstream.astype(jnp.float32) * out_block.astype(jnp.float32), axis=-1)
            )[:, :, None]
            grad_scores = (probability * (grad_probs - row_dot) * scale).astype(jnp.bfloat16)
            block_query.append(
                jnp.einsum(
                    "gqt,td->qgd", grad_scores, key_block, preferred_element_type=jnp.float32
                ).reshape(block_rows, group_cols)
            )
            key_sum = jnp.einsum(
                "gqt,qgd->td", grad_scores, query_block, preferred_element_type=jnp.float32
            )
            value_sum = jnp.einsum(
                "gqt,qgd->td", weights_b, upstream, preferred_element_type=jnp.float32
            )
        head_query.append(block_query[0])
        head_key.append(key_sum)
        head_value.append(value_sum)
    query_grads = jnp.concatenate(head_query, axis=1)
    key_grads = [jnp.concatenate(head_key, axis=1)]
    value_grads = [jnp.concatenate(head_value, axis=1)]
    key_grad_own, value_grad_own = (
        lax.psum_scatter(jnp.stack(key_grads), "context", scatter_dimension=1, tiled=True),
        lax.psum_scatter(jnp.stack(value_grads), "context", scatter_dimension=1, tiled=True),
    )
    grad_query_b = (
        rotate(query_grads.reshape(row_count, heads_dev, HEAD), cosine, sine_part, -1.0)
        .astype(jnp.bfloat16)
        .reshape(row_count, heads_dev * HEAD)
    )
    grad_key_b = (
        rotate(key_grad_own.reshape(row_count, kv_dev, HEAD), cosine, sine_part, -1.0)
        .astype(jnp.bfloat16)
        .reshape(row_count, kv_dev * HEAD)
    )
    grad_value_b = value_grad_own.reshape(row_count, kv_dev * HEAD).astype(jnp.bfloat16)
    grad_query = contract(normed_one_b, grad_query_b, 0, 0)
    grad_key_value = contract(
        normed_one_b, jnp.concatenate([grad_key_b, grad_value_b], axis=1), 0, 0
    )
    attention_back = (
        contract(grad_query_b, query_full, 1, 1)
        + contract(grad_key_b, key_full, 1, 1)
        + contract(grad_value_b, value_full, 1, 1)
    )
    attention_back = attention_back.reshape(seq_count, local_rows, model_width)
    grad_normed_one = full_total(attention_back)
    back_one, gain_one_term = rms_backward(grad_normed_one, unit_one, inverse_one, gain_one)
    grad_input = own_rows(grad_residual + back_one, share_count)
    feed_shares = reduce_grads(feed_terms)
    attention_shares = reduce_grads((gain_one_term, grad_query, grad_key_value, grad_output))
    gain_one_total = attention_shares[0]
    gain_two_total = feed_shares[0]
    key_cols = grad_key_b.shape[1]
    grad_key = attention_shares[2][:, :key_cols]
    grad_value = attention_shares[2][:, key_cols:]
    return (
        layer_out,
        grad_input,
        gain_one_total,
        attention_shares[1],
        grad_key,
        grad_value,
        attention_shares[3],
        gain_two_total,
        feed_shares[1],
        feed_shares[2],
        feed_shares[3],
    )


def solution(mesh):
    placed = (
        P("shard", "context", None),
        P("shard", "context", None),
        P("shard", None),
        P("shard", "context"),
        P("shard"),
        P("shard", "tensor"),
        P("shard", "tensor"),
        P("shard", "tensor"),
        P("tensor", "shard"),
        P("shard"),
        P("shard", "tensor"),
        P("shard", "tensor"),
        P("tensor", "shard"),
    )
    return jax.shard_map(
        local,
        mesh=mesh,
        in_specs=placed,
        out_specs=(
            P("shard", ("context", "tensor"), None),
            P("shard", ("context", "tensor"), None),
            P("shard"),
            P("shard", "tensor"),
            P("shard", "tensor"),
            P("shard", "tensor"),
            P("tensor", "shard"),
            P("shard"),
            P("shard", "tensor"),
            P("shard", "tensor"),
            P("tensor", "shard"),
        ),
        check_vma=False,
    )
```

profile of v0, /device:TPU:0, one launch (start us, length us, event | category | flops | bytes accessed | tf_op | source)
XLA Modules:
  0.0 1744.0 jit_solution(11127031290296175902)
XLA Ops:
  11.5 13.7 all-gather.1
  25.3 22.4 %all_gather.45 = bf16[2048,128]{1,0:T(8,128)(2,1)S(1)} all-gather(bf16[512,128]{1,0:T(8,128)(2,1)} %param.19), channel_id=1, replica_groups=mesh['shard'=4,'context'=2,'tensor'=4] {'shard'}, dimensions={0}, use_global_device_ids=true | all-gather | bytes 655360 | tf_op jit(solution)/shard_map/all_gather | solution.py:120
  49.2 5.6 all_gather.46
  54.9 20.7 %all_gather.43 = bf16[2048,128]{1,0:T(8,128)(2,1)S(1)} all-gather(bf16[512,128]{1,0:T(8,128)(2,1)} %param.20), channel_id=1, replica_groups=mesh['shard'=4,'context'=2,'tensor'=4] {'shard'}, dimensions={0}, use_global_device_ids=true | all-gather | bytes 655360 | tf_op jit(solution)/shard_map/all_gather | solution.py:121
  76.4 5.9 all-gather
  90.8 8.0 fusion.3
  103.1 7.7 fusion.2
  127.0 12.5 all-gather.2
  139.4 70.2 %all-reduce.11.cloned.1.call-done = f32[1,512,2048]{2,1,0:T(8,128)} async-done(((f32[1,512,2048]{2,1,0:T(8,128)}), f32[1,512,2048]{2,1,0:T(8,128)}) %all-reduce.11.cloned.1.call-update) | async-done | bytes 4194320 | tf_op jit(solution)/shard_map/psum | solution.py:68
  216.2 144.6 %all-gather.13.cloned.1.call-done = bf16[2048,2048]{1,0:T(8,128)(2,1)} async-done(((bf16[512,2048]{1,0:T(8,128)(2,1)}), bf16[2048,2048]{1,0:T(8,128)(2,1)}) %all-gather.13.cloned.1.call-update) | async-done | bytes 8388624 | tf_op jit(solution)/shard_map/all_gather | solution.py:124
  360.8 10.5 fusion.89
  371.3 138.7 %all-gather.15.cloned.1.call-done = bf16[2048,2048]{1,0:T(8,128)(2,1)} async-done(((bf16[512,2048]{1,0:T(8,128)(2,1)}), bf16[2048,2048]{1,0:T(8,128)(2,1)}) %all-gather.15.cloned.1.call-update) | async-done | bytes 8388624 | tf_op jit(solution)/shard_map/all_gather | solution.py:125
  510.1 10.5 fusion.90
  520.6 138.7 %all-gather.17.cloned.1.call-done = bf16[2048,2048]{1,0:T(8,128)(2,1)} async-done(((bf16[2048,512]{1,0:T(8,128)(2,1)}), bf16[2048,2048]{1,0:T(8,128)(2,1)}) %all-gather.17.cloned.1.call-update) | async-done | bytes 8388624 | tf_op jit(solution)/shard_map/all_gather | solution.py:126
  659.3 12.0 multiply_convert_fusion
  671.3 8.5 fusion.91
  679.9 6.1 add_bitcast_fusion.1
  686.3 83.6 %all-reduce.13.cloned.1.call-done = f32[1,512,2048]{2,1,0:T(8,128)} async-done(((f32[1,512,2048]{2,1,0:T(8,128)}), f32[1,512,2048]{2,1,0:T(8,128)}) %all-reduce.13.cloned.1.call-update) | async-done | bytes 4194320 | tf_op jit(solution)/shard_map/psum | solution.py:68
  806.1 16.4 reduce-scatter.11.cloned.1.call-done
  838.5 10.1 convolution_convert_fusion.2
  848.6 10.1 convolution_convert_fusion.1
  858.9 10.4 convolution_convert_fusion
  869.4 10.7 convolution_bitcast_fusion.1
  885.5 12.0 reduce-scatter.17.cloned.1.call-done
  897.4 45.0 %reduce-scatter.13.cloned.1.call-done = bf16[512,512]{1,0:T(8,128)(2,1)} async-done(((bf16[2048,512]{1,0:T(8,128)(2,1)}), bf16[512,512]{1,0:T(8,128)(2,1)}) %reduce-scatter.13.cloned.1.call-update) | async-done | bytes 524304 | tf_op jit(solution)/shard_map/reduce_scatter | solution.py:80
  942.4 146.2 %reduce-scatter.19.cloned.1.call-done = bf16[512,2048]{1,0:T(8,128)(2,1)} async-done(((bf16[2048,2048]{1,0:T(8,128)(2,1)}), bf16[512,2048]{1,0:T(8,128)(2,1)}) %reduce-scatter.19.cloned.1.call-update) | async-done | bytes 2097168 | tf_op jit(solution)/shard_map/reduce_scatter | solution.py:80
  1088.7 147.5 %reduce-scatter.21.cloned.1.call-done = bf16[512,2048]{1,0:T(8,128)(2,1)} async-done(((bf16[2048,2048]{1,0:T(8,128)(2,1)}), bf16[512,2048]{1,0:T(8,128)(2,1)}) %reduce-scatter.21.cloned.1.call-update) | async-done | bytes 2097168 | tf_op jit(solution)/shard_map/reduce_scatter | solution.py:83
  1236.1 147.5 %reduce-scatter.23.cloned.1.call-done = bf16[2048,512]{1,0:T(8,128)(2,1)} async-done(((bf16[2048,2048]{1,0:T(8,128)(2,1)}), bf16[2048,512]{1,0:T(8,128)(2,1)}) %reduce-scatter.23.cloned.1.call-update) | async-done | bytes 2097168 | tf_op jit(solution)/shard_map/reduce_scatter | solution.py:86
  1384.9 155.2 %all-reduce.15.cloned.1.call-done = (f32[1,512,2048]{2,1,0:T(8,128)}, f32[1,512,2048]{2,1,0:T(8,128)}) async-done(((f32[1,512,2048]{2,1,0:T(8,128)}, f32[1,512,2048]{2,1,0:T(8,128)}), (f32[1,512,2048]{2,1,0:T(8,128)}, f32[1,512,2048]{2,1,0:T(8,128)})) %all-reduce.15.cloned.1.call-update) | async-done | bytes 8388624 | tf_op jit(solution)/shard_map/psum | solution.py:68
  1540.1 6.6 multiply_reduce_fusion.1
  1546.7 11.8 all-reduce.3
  1569.0 155.8 %all-reduce.17.cloned.1.call-done = (bf16[512,512]{1,0:T(8,128)(2,1)}, bf16[512,256]{1,0:T(8,128)(2,1)}, bf16[512,512]{1,0:T(8,128)(2,1)}, bf16[512,2048]{1,0:T(...) async-done(((bf16[512,512]{1,0:T(8,128)(2,1)}, bf16[512,256]{1,0:T(8,128)(2,1)}, bf16[512,512]{1,0:T(8,128)(2,1)}, bf16[512,2048]{1,0:T(8,128)(2,1)}, ...) | async-done | bytes 7602192 | tf_op jit(solution)/shard_map/psum | solution.py:92
  (191 shorter events, 123.3 us)
Async XLA Ops:
  7.2 41.1 %copy-start.5 = (bf16[1,512,2048]{2,1,0:T(8,128)(2,1)S(1)}, bf16[1,512,2048]{2,1,0:T(8,128)(2,1)}, u32[]{:S(2)}) copy-start(bf16[1,512,2048]{2,1,0:T(8,128)(2,1)} %param.13) | copy-start | bytes 6291460
  7.2 40.7 %copy-start.30 = (s32[1,512]{1,0:T(1,128)S(1)}, s32[1,512]{1,0:T(1,128)}, u32[]{:S(2)}) copy-start(s32[1,512]{1,0:T(1,128)} %param.16) | copy-start | bytes 6148
  7.2 76.4 %all-gather.9.cloned.1.call-start = ((), (), s32[]{:S(2)}) async-start(), calls=%async_computation.8 | async-start | bytes 2621440 | tf_op jit(solution)/shard_map/all_gather | solution.py:119
  7.9 112.3 %all-gather.11.cloned.1.call-start = ((), (), s32[]{:S(2)}) async-start(), calls=%async_computation.9 | async-start | bytes 2621440 | tf_op jit(solution)/shard_map/all_gather | solution.py:122
  8.7 200.9 %all-reduce.11.cloned.1.call-start = ((), (), s32[]{:S(2)}) async-start(), calls=%async_computation.10 | async-start | bytes 8388608 | tf_op jit(solution)/shard_map/psum | solution.py:68
  47.7 27.9 %copy-start.9 = (bf16[2048,128]{1,0:T(8,128)(2,1)}, bf16[2048,128]{1,0:T(8,128)(2,1)S(1)}, u32[]{:S(2)}) copy-start(bf16[2048,128]{1,0:T(8,128)(2,1)S(1)} %all_gather.45) | copy-start | bytes 1572868
  49.2 33.2 %copy-start.29 = (s32[1,1024]{1,0:T(1,128)S(1)}, s32[1,1024]{1,0:T(1,128)}, u32[]{:S(2)}) copy-start(s32[1,1024]{1,0:T(1,128)} %param.15) | copy-start | bytes 12292
  54.9 48.2 %copy-start.16 = (bf16[1,1024,128]{1,2,0:T(8,128)(2,1)}, bf16[1,1024,128]{1,2,0:T(8,128)(2,1)S(1)}, u32[]{:S(2)}) copy-start(bf16[1,1024,128]{1,2,0:T(8,128)(2,1)S(1)} %all_gather.46) | copy-start | bytes 786436
  90.7 8.0 copy-start.20
  90.8 12.3 copy-start.18
  125.2 235.7 %all-gather.13.cloned.1.call-start = ((), (), s32[]{:S(2)}) async-start(), calls=%async_computation.11 | async-start | bytes 10485760 | tf_op jit(solution)/shard_map/all_gather | solution.py:124
  125.7 384.3 %all-gather.15.cloned.1.call-start = ((), (), s32[]{:S(2)}) async-start(), calls=%async_computation.12 | async-start | bytes 10485760 | tf_op jit(solution)/shard_map/all_gather | solution.py:125
  126.3 533.0 %all-gather.17.cloned.1.call-start = ((), (), s32[]{:S(2)}) async-start(), calls=%async_computation.13 | async-start | bytes 10485760 | tf_op jit(solution)/shard_map/all_gather | solution.py:126
  126.9 643.0 %all-reduce.13.cloned.1.call-start = ((), (), s32[]{:S(2)}) async-start(), calls=%async_computation.14 | async-start | bytes 8388608 | tf_op jit(solution)/shard_map/psum | solution.py:68
  671.3 8.5 copy-start.35
  671.3 8.6 copy-start.34
  671.3 8.6 copy-start.32
  686.0 119.0 %reduce-scatter.9.cloned.1.call-start = ((), (), s32[]{:S(2)}) async-start(), calls=%async_computation.15 | async-start | bytes 786432 | tf_op jit(solution)/shard_map/reduce_scatter | solution.py:304
  769.9 5.9 copy-start.6
  774.4 6.4 slice-start
  790.1 32.4 %reduce-scatter.11.cloned.1.call-start = ((), (), s32[]{:S(2)}) async-start(), calls=%async_computation.16 | async-start | bytes 786432 | tf_op jit(solution)/shard_map/reduce_scatter | solution.py:305
  800.8 84.7 %reduce-scatter.15.cloned.1.call-start = ((), (), s32[]{:S(2)}) async-start(), calls=%async_computation.18 | async-start | bytes 1310720 | tf_op jit(solution)/shard_map/reduce_scatter | solution.py:83
  806.1 19.4 %copy-start.27 = (bf16[512,2,64]{0,2,1:T(8,128)(2,1)}, bf16[512,2,64]{0,2,1:T(8,128)(2,1)S(1)}, u32[]{:S(2)}) copy-start(bf16[512,2,64]{0,2,1:T(8,128)(2,1)S(1)} %pad_maximum_fusion.6) | copy-start | bytes 393220
  825.5 71.9 %reduce-scatter.17.cloned.1.call-start = ((), (), s32[]{:S(2)}) async-start(), calls=%async_computation.19 | async-start | bytes 2621440 | tf_op jit(solution)/shard_map/reduce_scatter | solution.py:86
  830.4 112.0 %reduce-scatter.13.cloned.1.call-start = ((), (), s32[]{:S(2)}) async-start(), calls=%async_computation.17 | async-start | bytes 2621440 | tf_op jit(solution)/shard_map/reduce_scatter | solution.py:80
  838.4 250.2 %reduce-scatter.19.cloned.1.call-start = ((), (), s32[]{:S(2)}) async-start(), calls=%async_computation.20 | async-start | bytes 10485760 | tf_op jit(solution)/shard_map/reduce_scatter | solution.py:80
  848.5 387.6 %reduce-scatter.21.cloned.1.call-start = ((), (), s32[]{:S(2)}) async-start(), calls=%async_computation.21 | async-start | bytes 10485760 | tf_op jit(solution)/shard_map/reduce_scatter | solution.py:83
  858.7 524.9 %reduce-scatter.23.cloned.1.call-start = ((), (), s32[]{:S(2)}) async-start(), calls=%async_computation.22 | async-start | bytes 10485760 | tf_op jit(solution)/shard_map/reduce_scatter | solution.py:86
  869.3 670.8 %all-reduce.15.cloned.1.call-start = ((), (), s32[]{:S(2)}) async-start(), calls=%async_computation.23 | async-start | bytes 16777216 | tf_op jit(solution)/shard_map/psum | solution.py:68
  869.4 10.7 copy-start.7
  885.4 498.3 %copy-start.33 = (u32[32]{0:T(128)S(1)}, u32[32]{0:T(128)}, u32[]{:S(2)}) copy-start(u32[32]{0:T(128)} %constant.50) | copy-start | bytes 388
  885.4 839.5 %all-reduce.17.cloned.1.call-start = ((), (), s32[]{:S(2)}) async-start(), calls=%async_computation.24 | async-start | bytes 15204352 | tf_op jit(solution)/shard_map/psum | solution.py:92
  (25 other events, 70.4 us)
Sparse Core Ops, SparseCore 0:
  9.6 64.8 all-gather.8
  76.0 44.1 all-gather.10
  125.3 84.2 all-reduce.10
  211.0 149.7 all-gather.12
  362.2 147.7 all-gather.14
  511.5 147.7 all-gather.16
  686.2 83.6 all-reduce.12
  790.2 14.7 reduce-scatter.8
  807.9 14.6 reduce-scatter.10
  825.6 27.3 reduce-scatter.14
  855.3 42.1 reduce-scatter.16
  899.6 42.8 reduce-scatter.12
  944.8 143.8 reduce-scatter.18
  1090.9 145.2 reduce-scatter.20
  1238.3 145.2 reduce-scatter.22
  1386.6 153.4 all-reduce.14
  1542.9 181.8 all-reduce.16
where the time goes:
time: 1750 us; the launch traced here: 1740 us
  waiting for transfers between devices  1410 us (81%)
  matrix products  158 us (9%)
  blocking collectives  97.8 us (6%)
  other arithmetic  43.4 us (2%)
    psum x3, waiting for transfers between devices, full_total(): return lax.psum(partial_value, 'tensor')  309 us
    reduce_scatter x2, waiting for transfers between devices, reduce_grads(): lax.psum_scatter(terms[1].astype(jnp.bfloat16), 'shard', scatter_dimensio...  191 us
    reduce_scatter x2, waiting for transfers between devices, reduce_grads(): lax.psum_scatter(terms[3].astype(jnp.bfloat16), 'shard', scatter_dimensio...  159 us
    psum x1, waiting for transfers between devices, reduce_grads(): lax.psum(shares[1].astype(jnp.bfloat16), 'context').astype(jnp.float32)  156 us
    reduce_scatter x2, waiting for transfers between devices, reduce_grads(): lax.psum_scatter(terms[2].astype(jnp.bfloat16), 'shard', scatter_dimensio...  147 us
    all_gather x1, waiting for transfers between devices, local(): lax.all_gather(gate_weight, 'shard', axis=0, tiled=True)  145 us
    all_gather x1, waiting for transfers between devices, local(): lax.all_gather(down_weight, 'shard', axis=1, tiled=True)  139 us
    all_gather x1, waiting for transfers between devices, local(): lax.all_gather(up_weight, 'shard', axis=0, tiled=True)  139 us
  transfers between devices with their start and end apart: 17, of which 15 were waited for; matrix products, arithmetic and copies ran while one was open for 8% of the time, Pallas kernels for 0%

commit v1 on v0

v1 whole, which is shorter than its diff:
```python
import math

import jax
import jax.numpy as jnp
from jax import lax
from jax.experimental import pallas as pl
from jax.experimental.pallas import tpu as pltpu
from jax.sharding import PartitionSpec as P


HEAD = 64
NORM_EPS = 1e-05
ROPE_BASE = 500000.0
MASKED = -1e30
BF = jnp.bfloat16
SH, CX, TN = "shard", "context", "tensor"
F32 = jnp.float32


def contract(left, right, left_dim, right_dim):
    return lax.dot_general(
        left, right, (((left_dim,), (right_dim,)), ((), ())), preferred_element_type=F32
    )


def xor_bits(size):
    bits = []
    bit = 1
    while bit < size:
        bits.append(bit)
        bit *= 2
    assert bit == size
    return bits


def xor_offsets(size):
    offsets = [0]
    for bit in reversed(xor_bits(size)):
        offsets = offsets + [o ^ bit for o in offsets]
    return offsets


def swap(value, axis, offset):
    size = lax.axis_size(axis)
    return lax.ppermute(value, axis, [(i, i ^ offset) for i in range(size)])


def shift(value, steps):
    size = lax.axis_size(SH)
    return lax.ppermute(value, SH, [(i, (i + steps) % size) for i in range(size)])


def after(value, *others):
    return lax.optimization_barrier((value,) + others)[0]


def gather_direct(value):
    return [value] + [swap(value, CX, o) for o in xor_offsets(lax.axis_size(CX))[1:]]


def turn_blocks(value, dim):
    count = lax.axis_size(SH)
    me = lax.axis_index(SH)
    size = value.shape[dim] // count
    return jnp.concatenate(
        [
            lax.dynamic_slice_in_dim(value, ((me - b) % count) * size, size, dim)
            for b in range(count)
        ],
        axis=dim,
    )


def own_part(value, axis, dim, offset=0):
    count = lax.axis_size(axis)
    size = value.shape[dim] // count
    return lax.dynamic_slice_in_dim(value, (lax.axis_index(axis) ^ offset) * size, size, dim)


def gain_total(vectors):
    for axis in (TN, CX):
        for bit in xor_bits(lax.axis_size(axis)):
            vectors = vectors + swap(vectors, axis, bit)
    count = lax.axis_size(SH)
    me = lax.axis_index(SH)
    size = vectors.shape[1] // count
    total = lax.dynamic_slice_in_dim(vectors, me * size, size, 1)
    for r in range(1, count):
        part = lax.dynamic_slice_in_dim(vectors, ((me + r) % count) * size, size, 1)
        total = total + shift(part, r)
    return total


def whole(count):
    return [pl.BlockSpec(memory_space=pl.ANY)] * count


def params():
    return pltpu.CompilerParams(vmem_limit_bytes=56 * 1024 * 1024)


def mlp_kernel(first, r, n, k, m, refs):
    place, refs = refs[0], refs[1:]
    heads = k if r else 2 * k
    acts, cots, weights = refs[:k], refs[k:heads], refs[heads : heads + n * m]
    kept = 2 + 2 * m
    rest = refs[heads + n * m + (0 if first else kept) :]
    all_acts, all_cots, all_hid, all_back = rest[0], rest[1], rest[2 : 2 + m], rest[2 + m : kept]
    low, high = rest[kept : kept + 2]
    a_v, c_v, gu_v, d_v, hid_v, back_v, low_v, high_v, in_sem, out_sem = rest[kept + 2 :]
    rows, width = a_v.shape
    share, block = rows // k, width // n
    units = d_v.shape[2]
    here = pl.ds(r * rows, rows)
    gets = []

    def get(source, target):
        copy = pltpu.make_async_copy(source, target, in_sem.at[len(gets)])
        copy.start()
        gets.append(copy)
        return copy

    top, bottom = pl.ds(0, share), pl.ds(share, share)
    a_get = [get(acts[j].at[top], a_v.at[pl.ds(j * share, share)]) for j in range(k)]
    gu_get = [
        [get(weights[i * m + j].at[pl.ds(0, block)], gu_v.at[j, at(place, 1 + i, block)]) for i in range(n)]
        for j in range(m)
    ]
    c_get = [
        get(acts[j].at[bottom] if r else cots[j], c_v.at[pl.ds(j * share, share)]) for j in range(k)
    ]
    d_get = [
        [get(weights[i * m + j].at[pl.ds(block, units)], d_v.at[j, i]) for i in range(n)]
        for j in range(m)
    ]
    puts = []

    def put(source, target):
        copy = pltpu.make_async_copy(source, target, out_sem.at[len(puts)])
        copy.start()
        puts.append(copy)

    for copy in a_get:
        copy.wait()
    put(a_v, all_acts.at[here])
    pres = []
    for j in range(m):
        for copy in gu_get[j]:
            copy.wait()
        pres.append(jnp.dot(a_v[...], gu_v[j], preferred_element_type=F32))
    for copy in c_get:
        copy.wait()
    put(c_v, all_cots.at[here])
    for j in range(m):
        for copy in d_get[j]:
            copy.wait()
        gate, up = pres[j][:, :units], pres[j][:, units:]
        sig = 1.0 / (1.0 + jnp.exp(-gate))
        act = gate * sig
        hid_v[j] = (act * up).astype(BF)
        grad = 0.0
        for i in range(n):
            grad += contract(c_v[:, at(place, 1 + i, block)], d_v[j, i], 1, 1)
        gate_back = grad * up * sig * (1.0 + gate * (1.0 - sig))
        back_v[j, :, :units] = gate_back.astype(BF)
        back_v[j, :, units:] = (grad * act).astype(BF)
        put(hid_v.at[j], all_hid[j].at[here])
        put(back_v.at[j], all_back[j].at[here])
    half = rows // 2

    def grad_in(part):
        total = 0.0
        for j in range(m):
            total += contract(back_v[j, part, :], gu_v[j], 1, 1)
        return total

    high_v[...] = grad_in(slice(half, rows)).astype(BF)
    put(high_v, high)
    low_v[...] = grad_in(slice(0, half))
    put(low_v, low)
    for copy in puts:
        copy.wait()


def mlp_chunk(r, n, m, place, acts, cots, weights, carried):
    k = len(acts)
    width = acts[0].shape[1]
    share = acts[0].shape[0] // (2 if r else 1)
    rows, block = share * k, width // n
    units = weights[0].shape[1] // 2
    first = carried is None
    total = n * rows
    sizes = [width] * 2 + [units] * m + [2 * units] * m
    big = [jax.ShapeDtypeStruct((total, cols), BF) for cols in sizes]
    outs = big + [
        jax.ShapeDtypeStruct((rows // 2, width), F32),
        jax.ShapeDtypeStruct((rows // 2, width), BF),
    ]
    operands = [place] + list(acts) + list(cots) + list(weights)
    aliases = {}
    if not first:
        aliases = {len(operands) + i: i for i in range(len(big))}
        operands = operands + list(carried)
    res = pl.pallas_call(
        lambda *refs: mlp_kernel(first, r, n, k, m, refs),
        out_shape=outs,
        in_specs=[pl.BlockSpec(memory_space=pltpu.SMEM)] + whole(len(operands) - 1),
        out_specs=whole(len(outs)),
        input_output_aliases=aliases,
        scratch_shapes=[
            pltpu.VMEM((rows, width), BF),
            pltpu.VMEM((rows, width), BF),
            pltpu.VMEM((m, width, 2 * units), BF),
            pltpu.VMEM((m, n, units, block), BF),
            pltpu.VMEM((m, rows, units), BF),
            pltpu.VMEM((m, rows, 2 * units), BF),
            pltpu.VMEM((rows // 2, width), F32),
            pltpu.VMEM((rows // 2, width), BF),
            pltpu.SemaphoreType.DMA((2 * k + 2 * n * m,)),
            pltpu.SemaphoreType.DMA((4 + 2 * m,)),
        ],
        compiler_params=params(),
        name="mc",
    )(*operands)
    return res[: len(big)], res[-2], res[-1]


def feed_kernel(n, m, block, place, *refs):
    hid, weights, low, high = refs[:m], refs[m : m + n * m], refs[m + n * m], refs[m + n * m + 1]
    rows = hid[0].shape[1]
    half = rows // 2
    for i in range(n):
        total = 0.0
        for j in range(m):
            total += jnp.dot(hid[j][0], weights[i * m + j][block:, :], preferred_element_type=F32)
        low[0, :, at(place, 1 + i, block)] = total[:half].astype(BF)
        high[0, :, at(place, 1 + i, block)] = total[half:].astype(BF)


def feed_out(place, hid, weights, rows, n):
    m = len(hid)
    units = hid[0].shape[1]
    block = weights[0].shape[0] - units
    width = n * block
    out = jax.ShapeDtypeStruct((n, rows // 2, width), BF)
    return pl.pallas_call(
        lambda *refs: feed_kernel(n, m, block, *refs),
        grid=(n,),
        out_shape=[out, out],
        in_specs=[pl.BlockSpec(memory_space=pltpu.SMEM)]
        + [pl.BlockSpec((1, rows, units), lambda i: (i, 0, 0)) for _ in hid]
        + [pl.BlockSpec(w.shape, lambda i: (0, 0)) for w in weights],
        out_specs=[pl.BlockSpec((1, rows // 2, width), lambda i: (i, 0, 0))] * 2,
        compiler_params=params(),
        name="fo",
    )(place, *[h.reshape(n, rows, units) for h in hid], *weights)


def feed_add_kernel(place, low, received, kept, sent):
    half = kept.shape[0]
    total = low[0].astype(F32) + received[0].astype(F32)
    kept[...] = total[:half]
    sent[...] = total[half:].astype(BF)


def feed_add(place, low, received):
    n, rows, width = low.shape
    half = rows // 2
    part = pl.BlockSpec((None, half, width), lambda i: (i, 0, 0))
    full = pl.BlockSpec((1, rows, width), lambda i: (i, 0, 0))
    return pl.pallas_call(
        feed_add_kernel,
        grid=(n,),
        out_shape=[jax.ShapeDtypeStruct((n, half, width), t) for t in (F32, BF)],
        in_specs=[pl.BlockSpec(memory_space=pltpu.SMEM), full, full],
        out_specs=[part, part],
        compiler_params=params(),
        name="fa",
    )(place, low, received)


def spread_kernel(n, m, place, gate, up, down, *outs):
    me = place[0]
    rows, cols = gate.shape
    units = cols // n // m
    offsets = xor_offsets(m)

    def fill(out, source, want):
        low = pl.multiple_of(source * (m * units), m * units)
        for value, col in ((gate, 0), (up, units)):
            both = value[:, pl.ds(low, m * units)]
            chosen = both[:, :units]
            for index in range(1, m):
                chosen = jnp.where(want == index, both[:, index * units : (index + 1) * units], chosen)
            out[:rows, col : col + units] = chosen
        row = pl.multiple_of((source * m + want) * units, units)
        out[rows:, :] = down[pl.ds(row, units), :]

    for j in range(m):
        fill(outs[j], place[1], me ^ offsets[j])
    for r in range(1, n):
        fill(outs[m + r - 1], place[1 + n - r], me)


def spread_units(place, gate, up, down, n, m):
    rows, cols = gate.shape
    units = cols // n // m
    assert down.shape[1] == rows == 2 * units
    vmem = pl.BlockSpec(memory_space=pltpu.VMEM)
    return pl.pallas_call(
        lambda *refs: spread_kernel(n, m, *refs),
        out_shape=[jax.ShapeDtypeStruct((rows + units, 2 * units), BF)] * (m + n - 1),
        in_specs=[pl.BlockSpec(memory_space=pltpu.SMEM)] + [vmem] * 3,
        out_specs=[vmem] * (m + n - 1),
        compiler_params=params(),
        name="su",
    )(place, gate, up, down)


def unit_grad_kernel(count, place, acts, cots, hid, back, *outs):
    block = acts.shape[1]
    top = contract(acts[...], back[...], 0, 0)
    bottom = contract(hid[...], cots[...], 0, 0)
    for i in range(count):

        @pl.when(pl.program_id(0) == i)
        def _(out=outs[i]):
            out[:block, :] = top.astype(out.dtype)
            out[block:, :] = bottom.astype(out.dtype)


def unit_grads(place, acts, cots, hid, back, dtype, n, first, count):
    rows, width = acts.shape
    block, units = width // n, hid.shape[1]
    out = jax.ShapeDtypeStruct((block + units, 2 * units), dtype)
    cols = pl.BlockSpec((rows, block), lambda i, place: (0, place[1 + (first + i) % n]))

    def all_of(shape):
        return pl.BlockSpec(shape, lambda i, place: (0, 0))

    return list(
        pl.pallas_call(
            lambda *refs: unit_grad_kernel(count, *refs),
            out_shape=[out] * count,
            grid_spec=pltpu.PrefetchScalarGridSpec(
                num_scalar_prefetch=1,
                grid=(count,),
                in_specs=[cols, cols, all_of(hid.shape), all_of(back.shape)],
                out_specs=[all_of(out.shape)] * count,
            ),
            compiler_params=params(),
        )(place, acts, cots, hid, back)
    )


def join_kernel(r, n, m, first, place, *refs):
    pieces = refs[:m]
    gate, up, down, gate_v, up_v, down_v, sems = refs[m + (0 if first else 3) :]
    units = pieces[0].shape[1] // 2
    block = pieces[0].shape[0] - units
    me = place[0]
    offsets = xor_offsets(m)
    for index in range(m):
        chosen = pieces[0][...].astype(F32)
        for j in range(1, m):
            chosen = jnp.where((me ^ offsets[j]) == index, pieces[j][...].astype(F32), chosen)
        gate_v[:, index * units : (index + 1) * units] = chosen[:block, :units]
        up_v[:, index * units : (index + 1) * units] = chosen[:block, units:]
        down_v[index * units : (index + 1) * units, :] = chosen[block:, :]
    there = at(place, 1 + (n - r) % n, m * units)
    copies = [
        pltpu.make_async_copy(gate_v, gate.at[:, there], sems.at[0]),
        pltpu.make_async_copy(up_v, up.at[:, there], sems.at[1]),
        pltpu.make_async_copy(down_v, down.at[there], sems.at[2]),
    ]
    for copy in copies:
        copy.start()
    for copy in copies:
        copy.wait()


def join_units(place, r, n, pieces, carried):
    m = len(pieces)
    units = pieces[0].shape[1] // 2
    block = pieces[0].shape[0] - units
    total = n * m * units
    vmem = pl.BlockSpec(memory_space=pltpu.VMEM)
    operands = [place, *pieces] + (list(carried) if carried else [])
    return pl.pallas_call(
        lambda *refs: join_kernel(r, n, m, not carried, *refs),
        out_shape=[shaped((block, total), F32)] * 2 + [shaped((total, block), F32)],
        in_specs=[pl.BlockSpec(memory_space=pltpu.SMEM)] + [vmem] * m + whole(3 if carried else 0),
        out_specs=whole(3),
        input_output_aliases={1 + m + i: i for i in range(3)} if carried else {},
        scratch_shapes=[
            pltpu.VMEM((block, m * units), F32),
            pltpu.VMEM((block, m * units), F32),
            pltpu.VMEM((m * units, block), F32),
            pltpu.SemaphoreType.DMA((3,)),
        ],
        compiler_params=params(),
        name="ju",
    )(*operands)


def pick_kernel(m, offsets, place, *refs):
    weights, outs = refs[:3], refs[3:]
    me = place[0]
    for j in range(m):
        low = 0
        for w in weights:
            cols = w.shape[1] // m
            chosen = w[:, :cols]
            for index in range(1, m):
                chosen = jnp.where((me ^ offsets[j]) == index, w[:, index * cols : (index + 1) * cols], chosen)
            outs[j][:, low : low + cols] = chosen
            low += cols


def pick_parts(weights, m):
    rows = weights[0].shape[0]
    cols = sum(w.shape[1] for w in weights) // m
    me = lax.axis_index(CX).astype(jnp.int32).reshape(1)
    offsets = xor_offsets(m)
    return pl.pallas_call(
        lambda *refs: pick_kernel(m, offsets, *refs),
        out_shape=[jax.ShapeDtypeStruct((rows, cols), BF)] * m,
        in_specs=[pl.BlockSpec(memory_space=pltpu.SMEM)] + [pl.BlockSpec(memory_space=pltpu.VMEM)] * 3,
        out_specs=[pl.BlockSpec(memory_space=pltpu.VMEM)] * m,
        compiler_params=params(),
        name="pp",
    )(me, *weights)


def join_rows_kernel(m, offsets, place, *refs):
    pieces, out = refs[:m], refs[m]
    n, units, _ = pieces[0].shape
    me = place[0]
    for b in range(n):
        for index in range(m):
            chosen = pieces[0][b].astype(F32)
            for j in range(1, m):
                chosen = jnp.where((me ^ offsets[j]) == index, pieces[j][b].astype(F32), chosen)
            low = (b * m + index) * units
            out[low : low + units, :] = chosen


def join_rows(pieces):
    m = len(pieces)
    n, units, cols = pieces[0].shape
    me = lax.axis_index(CX).astype(jnp.int32).reshape(1)
    offsets = xor_offsets(m)
    return pl.pallas_call(
        lambda *refs: join_rows_kernel(m, offsets, *refs),
        out_shape=jax.ShapeDtypeStruct((n * m * units, cols), F32),
        in_specs=[pl.BlockSpec(memory_space=pltpu.SMEM)] + [pl.BlockSpec(memory_space=pltpu.VMEM)] * m,
        out_specs=pl.BlockSpec(memory_space=pltpu.VMEM),
        compiler_params=params(),
        name="jr",
    )(me, *pieces)


def scalars(*values):
    return jnp.stack([jnp.asarray(v, jnp.int32) for v in values])


def call(kernel, outs, operands, scratch=()):
    vmem = pl.BlockSpec(memory_space=pltpu.VMEM)
    return pl.pallas_call(
        kernel,
        out_shape=outs,
        in_specs=[pl.BlockSpec(memory_space=pltpu.SMEM)] + [vmem] * (len(operands) - 1),
        out_specs=jax.tree.map(lambda _: vmem, outs),
        scratch_shapes=scratch,
        compiler_params=params(),
    )(*operands)


def shaped(shape, dtype):
    return jax.ShapeDtypeStruct(shape, dtype)


def at(base, index, size):
    return pl.ds(pl.multiple_of(base[index] * size, size), size)


def norm_kernel(n, k, place, hidden, gains, out):
    rows = hidden.shape[0]
    share = rows // k
    gain = gains[0:1, :].astype(F32)
    for j in range(k):
        x = hidden[at(place, 1 + n + j, share), :].astype(F32)
        inverse = lax.rsqrt(jnp.mean(x * x, axis=-1, keepdims=True) + NORM_EPS)
        out[j * share : (j + 1) * share, :] = (x * inverse * gain).astype(BF)


def turn_heads(u, cosine, sine, turn):
    width = u.shape[1]
    half = HEAD // 2
    place = lax.broadcasted_iota(jnp.int32, u.shape, 1) % HEAD
    other = jnp.where(place < half, pltpu.roll(u, width - half, 1), pltpu.roll(u, half, 1))
    reps = width // cosine.shape[1]
    cos_all = jnp.concatenate([cosine] * reps, axis=1) if reps > 1 else cosine
    sin_all = jnp.concatenate([sine] * reps, axis=1) if reps > 1 else sine
    return u * cos_all + turn * other * sin_all


def qkv_kernel(n, m, q_cols, kv_cols, place, normed, cosine, sine, *refs):
    weights, query, kv_own, kv_sends = refs[: n * m], refs[n * m], refs[n * m + 1], refs[n * m + 2 :]
    block = normed.shape[1] // n
    totals = []
    for j in range(m):
        total = 0.0
        for r in range(n):
            x = normed[:, at(place, 1 + r, block)]
            total += jnp.dot(x, weights[r * m + j][...], preferred_element_type=F32)
        totals.append(total)
    cos, sin = cosine[...], sine[...]
    for j in range(m):
        turned = turn_heads(totals[j][:, :q_cols], cos, sin, 1.0)
        query[:, j * q_cols : (j + 1) * q_cols] = turned.astype(BF)
    keys = jnp.concatenate([t[:, q_cols : q_cols + kv_cols] for t in totals], axis=1)
    keys = turn_heads(keys, cos, sin, 1.0).astype(BF)
    keys = [keys[:, j * kv_cols : (j + 1) * kv_cols] for j in range(m)]
    values = [t[:, q_cols + kv_cols :].astype(BF) for t in totals]
    offsets = xor_offsets(m)
    for o, out in zip(offsets, (kv_own,) + tuple(kv_sends)):
        order = [offsets.index(p ^ o) for p in offsets]
        out[...] = jnp.concatenate([keys[j] for j in order] + [values[j] for j in order], axis=1)


def mask_bias(n, k, rows, place, seg_row, seg_col, order):
    share = rows // k
    me = place[0]
    blocks = []
    q_seg = []
    q_place = []
    step = lax.broadcasted_iota(jnp.int32, (share, 1), 0)
    lane = lax.broadcasted_iota(jnp.int32, (1, share), 1)
    for j in range(k):
        base = pl.multiple_of(me * rows + place[1 + n + j] * share, share)
        q_seg.append(seg_col[pl.ds(base, share), :])
        q_place.append(step + base)
    q_seg = jnp.concatenate(q_seg, axis=0)
    q_place = jnp.concatenate(q_place, axis=0)
    for o in order:
        for j in range(k):
            base = pl.multiple_of((me ^ o) * rows + place[1 + n + j] * share, share)
            k_seg = seg_row[:, pl.ds(base, share)]
            seen = (q_place >= lane + base) & (q_seg == k_seg)
            blocks.append(jnp.where(seen, 0.0, MASKED))
    return jnp.concatenate(blocks, axis=1)


def attend_kernel(n, m, k, place, query, seg_row, seg_col, kv_own, *refs):
    kv, attended, totals = (kv_own,) + refs[: m - 1], refs[m - 1], refs[m]
    bias_v, keys_v = refs[m + 1], refs[m + 2]
    rows, q_width = query.shape
    kv_width = kv_own.shape[1] // 2
    heads, kv_heads = q_width // HEAD, kv_width // HEAD
    group = heads // kv_heads
    bias_v[...] = mask_bias(n, k, rows, place, seg_row, seg_col, xor_offsets(m))
    for i in range(m):
        keys_v[i * rows : (i + 1) * rows, :] = kv[i][...]
    lanes = lax.broadcasted_iota(jnp.int32, totals.shape, 1)
    kept = jnp.zeros(totals.shape, F32)
    for h in range(heads):
        g = h // group
        q = query[:, h * HEAD : (h + 1) * HEAD] * (1.0 / math.sqrt(HEAD))
        scores = contract(q.astype(BF), keys_v[:, g * HEAD : (g + 1) * HEAD], 1, 1) + bias_v[...]
        log_total = jnp.log(jnp.sum(jnp.exp(scores), axis=1, keepdims=True))
        prob = jnp.exp(scores - log_total).astype(BF)
        value = keys_v[:, kv_width + g * HEAD : kv_width + (g + 1) * HEAD]
        out = jnp.dot(prob, value, preferred_element_type=F32)
        attended[:, h * HEAD : (h + 1) * HEAD] = out.astype(BF)
        kept = jnp.where(lanes == h, log_total, kept)
    totals[...] = kept


def out_weight(m, place, out_w, firsts, others, r, j):
    part = out_w.shape[0] // m
    if r == 0:
        row = pl.multiple_of((place[0] ^ xor_offsets(m)[j]) * part, part)
        return out_w[pl.ds(row, part), :]
    if j == 0:
        return firsts[r - 1][...]
    return others[j - 1][r - 1]


def out_kernel(n, m, place, attended, out_w, *refs):
    firsts, others = refs[: n - 1], refs[n - 1 : n + m - 2]
    low, high = refs[n + m - 2 :]
    rows, cols = attended.shape
    part, half = cols // m, rows // 2
    block = out_w.shape[1]
    for r in range(n):
        total = 0.0
        for j in range(m):
            w = out_weight(m, place, out_w, firsts, others, r, j)
            total += jnp.dot(attended[:, j * part : (j + 1) * part], w, preferred_element_type=F32)
        low[:, at(place, 1 + r, block)] = total[:half]
        high[:, at(place, 1 + r, block)] = total[half:].astype(BF)


def residual_kernel(place, kept, received, hidden, gains, cot, residual, normed, stream):
    share = kept.shape[0]
    total = hidden[...].astype(F32) + (kept[...] + received[...].astype(F32))
    inverse = lax.rsqrt(jnp.mean(total * total, axis=-1, keepdims=True) + NORM_EPS)
    residual[...] = total
    result = (total * inverse * gains[1:2, :].astype(F32)).astype(BF)
    normed[...] = result
    stream[:share, :] = result
    stream[share:, :] = cot[...]


def norm_back(upstream, values, gain):
    inverse = lax.rsqrt(jnp.mean(values * values, axis=-1, keepdims=True) + NORM_EPS)
    unit = values * inverse
    scaled = upstream * gain
    result = inverse * (scaled - unit * jnp.mean(scaled * unit, axis=-1, keepdims=True))
    return result, jnp.sum(upstream * unit, axis=0, keepdims=True)


def feed_back_kernel(place, kept, received, residual, gains, cot, *refs):
    moved, grad, grad_b, gain_term = refs[:-3], *refs[-3:]
    upstream = kept[...] + received[...].astype(F32)
    for part in moved:
        upstream += part[...].astype(F32)
    result, term = norm_back(upstream, residual[...], gains[1:2, :].astype(F32))
    result += cot[...].astype(F32)
    grad[...] = result
    grad_b[...] = result.astype(BF)
    gain_term[...] = term


def input_back_kernel(place, kept, received, hidden, gains, grad_residual, out, gain_term):
    x = hidden[...].astype(F32)
    upstream = kept[...] + received[...].astype(F32)
    result, term = norm_back(upstream, x, gains[0:1, :].astype(F32))
    out[...] = grad_residual[...] + result
    gain_term[...] = term


def out_back_kernel(n, m, k, place, out_w, *refs):
    grads, refs = refs[:k], refs[k:]
    firsts, others = refs[: n - 1], refs[n - 1 : n + m - 2]
    attended_grad, grads_v = refs[n + m - 2 :]
    share, width = grads[0].shape
    block = width // n
    part = attended_grad.shape[1] // m
    for i in range(k):
        grads_v[i * share : (i + 1) * share, :] = grads[i][...]
    for j in range(m):
        total = 0.0
        for r in range(n):
            w = out_weight(m, place, out_w, firsts, others, r, j)
            total += contract(grads_v[:, at(place, 1 + r, block)], w, 1, 1)
        attended_grad[:, j * part : (j + 1) * part] = total.astype(BF)


def out_grad_kernel(n, m, place, attended, grads, *outs):
    part, block = attended.shape[1] // m, grads.shape[1] // n
    for j in reversed(range(m)):
        for r in range(n):
            total = contract(attended[:, j * part : (j + 1) * part], grads[:, at(place, 1 + r, block)], 0, 0)
            outs[r][j * part : (j + 1) * part, :] = total.astype(outs[r].dtype)


def attend_back_kernel(n, m, k, place, query, seg_row, seg_col, attended, upstream, totals, kv_own, *refs):
    kv, refs = (kv_own,) + refs[: m - 1], refs[m - 1 :]
    query_grad, kv_grad, kv_sends = refs[0], refs[1], refs[2 : 1 + m]
    bias_v, keys_v, grads_v = refs[1 + m :]
    rows, q_width = query.shape
    kv_width = kv_own.shape[1] // 2
    heads, kv_heads = q_width // HEAD, kv_width // HEAD
    group = heads // kv_heads
    scale = 1.0 / math.sqrt(HEAD)
    offsets = xor_offsets(m)
    bias_v[...] = mask_bias(n, k, rows, place, seg_row, seg_col, offsets)
    for i in range(m):
        keys_v[i * rows : (i + 1) * rows, :] = kv[i][...]
    for g in range(kv_heads):
        key = keys_v[:, g * HEAD : (g + 1) * HEAD]
        value = keys_v[:, kv_width + g * HEAD : kv_width + (g + 1) * HEAD]
        key_sum, value_sum = 0.0, 0.0
        for h in range(g * group, (g + 1) * group):
            cols = slice(h * HEAD, (h + 1) * HEAD)
            q, up = query[:, cols], upstream[:, cols]
            row_dot = jnp.sum(up.astype(F32) * attended[:, cols].astype(F32), axis=1, keepdims=True)
            scores = contract((q * scale).astype(BF), key, 1, 1) + bias_v[...]
            prob = jnp.exp(scores - totals[:, h : h + 1])
            grad_prob = contract(up, value, 1, 1)
            grad_scores = (prob * ((grad_prob - row_dot) * scale)).astype(BF)
            query_grad[:, cols] = jnp.dot(grad_scores, key, preferred_element_type=F32)
            key_sum += contract(grad_scores, q, 0, 0)
            value_sum += contract(prob.astype(BF), up, 0, 0)
        grads_v[:, g * HEAD : (g + 1) * HEAD] = key_sum
        grads_v[:, kv_width + g * HEAD : kv_width + (g + 1) * HEAD] = value_sum
    kv_grad[...] = grads_v[:rows, :]
    cols = kv_width // m
    for i in range(1, m):
        here = grads_v[i * rows : (i + 1) * rows, :]
        order = [offsets.index(p ^ offsets[i]) for p in offsets]
        pieces = [here[:, low + j * cols : low + (j + 1) * cols] for low in (0, kv_width) for j in order]
        kv_sends[i - 1][...] = jnp.concatenate(pieces, axis=1).astype(BF)


def join_grads_kernel(m, q_cols, kv_cols, place, query_grad, kv_grad, cosine, sine, *refs):
    received, outs = refs[: m - 1], refs[m - 1 :]
    kv_width = m * kv_cols
    cos, sin = cosine[...], sine[...]
    total = kv_grad[...]
    for piece in received:
        total += piece[...].astype(F32)
    keys = turn_heads(total[:, :kv_width], cos, sin, -1.0).astype(BF)
    values = total[:, kv_width:].astype(BF)
    for j in range(m):
        turned = turn_heads(query_grad[:, j * q_cols : (j + 1) * q_cols], cos, sin, -1.0)
        outs[j][:, :q_cols] = turned.astype(BF)
        outs[j][:, q_cols : q_cols + kv_cols] = keys[:, j * kv_cols : (j + 1) * kv_cols]
        outs[j][:, q_cols + kv_cols :] = values[:, j * kv_cols : (j + 1) * kv_cols]


def qkv_grad_kernel(n, place, normed, grads, *outs):
    block = normed.shape[1] // n
    for i in range(n):
        r = (1 + i) % n
        total = contract(normed[:, at(place, 1 + r, block)], grads[...], 0, 0)
        outs[r][...] = total.astype(outs[r].dtype)


def qkv_back_kernel(n, m, place, *refs):
    grads, weights, low, high = refs[:m], refs[m : m + n * m], refs[m + n * m], refs[m + n * m + 1]
    block = low.shape[1] // n
    half = low.shape[0]
    for r in range(n):
        total = 0.0
        for j in range(m):
            total += contract(grads[j][...], weights[r * m + j][...], 1, 1)
        low[:, at(place, 1 + r, block)] = total[:half]
        high[:, at(place, 1 + r, block)] = total[half:].astype(BF)


def qkv_join_kernel(m, offsets, q_cols, kv_cols, place, *refs):
    pieces, outs = refs[:m], refs[m:]
    me = place[0]
    for index in range(m):
        chosen = pieces[0][...].astype(F32)
        for j in range(1, m):
            chosen = jnp.where((me ^ offsets[j]) == index, pieces[j][...].astype(F32), chosen)
        low = 0
        for out, cols in zip(outs, (q_cols, kv_cols, kv_cols)):
            out[:, index * cols : (index + 1) * cols] = chosen[:, low : low + cols]
            low += cols


def local(
    hidden_in,
    cotangent,
    segment_ids,
    positions,
    attention_gain,
    query_weight,
    key_weight,
    value_weight,
    output_weight,
    feed_gain,
    gate_weight,
    up_weight,
    down_weight,
):
    n = lax.axis_size(SH)
    m = lax.axis_size(CX)
    k = lax.axis_size(TN)
    shard = lax.axis_index(SH)
    ctx = lax.axis_index(CX)
    ten = lax.axis_index(TN)
    t_offsets = xor_offsets(k)
    c_offsets = xor_offsets(m)
    _, rows, width = hidden_in.shape
    share = rows // k
    block = width // n
    place = scalars(ctx, *[(shard - r) % n for r in range(n)], *[ten ^ o for o in t_offsets])
    hidden, cot = hidden_in[0], cotangent[0]

    kv_part = key_weight.shape[1] // HEAD // m
    q_cols = query_weight.shape[1] // m
    kv_cols = kv_part * HEAD
    part_cols = q_cols + 2 * kv_cols
    qkv_parts = pick_parts((query_weight, key_weight, value_weight), m)
    qkv_w = [qkv_parts]
    piece = qkv_parts[0]
    for r in range(1, n):
        piece = shift(piece, 1)
        qkv_w.append(gather_direct(piece))
        if r == max(n - 2, 1):
            middle_piece = piece
    if n == 1:
        middle_piece = piece
    gains = after(jnp.stack([attention_gain, feed_gain]), qkv_parts[0])
    gains = turn_blocks(jnp.concatenate([gains] + [shift(gains, r) for r in range(1, n)], axis=1), 1)

    units_mine = spread_units(place, gate_weight, up_weight, down_weight, n, m)
    unit_w = [list(units_mine[:m])]
    cot_pieces = [
        lax.dynamic_slice_in_dim(cot, (ten ^ o) * share, share, 0) for o in t_offsets
    ]
    hidden_own = own_part(hidden, TN, 0)
    out_mine = own_part(output_weight, CX, 0)
    inverse_freq = ROPE_BASE ** (-(jnp.arange(HEAD // 2, dtype=F32) * 2.0 / HEAD))
    place_rows = jnp.concatenate(
        [lax.dynamic_slice_in_dim(positions[0], (ten ^ o) * share, share, 0) for o in t_offsets]
    )
    reps = m * kv_cols // (HEAD // 2)
    angles = place_rows.astype(F32)[:, None] * jnp.tile(inverse_freq, reps)[None, :]
    signs = jnp.tile(jnp.repeat(jnp.array([-1.0, 1.0], F32), HEAD // 2), reps // 2)
    cosine, sine = jnp.cos(angles), jnp.sin(angles) * signs[None, :]
    seg_row = segment_ids
    seg_col = segment_ids.reshape(-1, 1)

    normed_one = call(
        lambda *refs: norm_kernel(n, k, *refs), shaped((rows, width), BF), (place, hidden, gains)
    )
    out_mine = after(out_mine, middle_piece)
    out_firsts = []
    for r in range(1, n):
        out_firsts.append(shift(out_mine, r))
    flat_qkv = [w for parts in qkv_w for w in parts]
    query, kv_own, *kv_sends = call(
        lambda *refs: qkv_kernel(n, m, q_cols, kv_cols, *refs),
        [shaped((rows, m * q_cols), BF)] + [shaped((rows, 2 * m * kv_cols), BF)] * m,
        (place, normed_one, cosine, sine, *flat_qkv),
    )
    early_values = lax.optimization_barrier((kv_own, hidden_own, *cot_pieces, seg_col, middle_piece))
    kv_own, hidden_own, cot_pieces, seg_col = (
        early_values[0],
        early_values[1],
        list(early_values[2 : 2 + k]),
        early_values[2 + k],
    )
    kv_others = []
    for o, sent in zip(c_offsets[1:], kv_sends):
        kv_others.append(swap(sent, CX, o))
    out_stack = after(jnp.stack(out_firsts), kv_own)
    out_others = []
    for o in c_offsets[1:]:
        out_others.append(swap(out_stack, CX, o))
    units_sent = list(units_mine[m:])
    early = [r for r in range(1, n) if r != n // 2]
    moved = [None] * n
    for r in early:
        moved[r] = shift(units_sent[r - 1] if r == 1 else after(units_sent[r - 1], out_stack), r)
    wide = 2 * m * kv_cols
    attended, totals = call(
        lambda *refs: attend_kernel(n, m, k, *refs),
        [shaped((rows, m * q_cols), BF), shaped((rows, 128), F32)],
        (place, query, seg_row, seg_col, kv_own, *kv_others),
        [pltpu.VMEM((rows, m * rows), F32), pltpu.VMEM((m * rows, wide), BF)],
    )
    for r in range(1, n):
        if r not in early:
            moved[r] = shift(after(units_sent[r - 1], attended), r)
    low, high = call(
        lambda *refs: out_kernel(n, m, *refs),
        [shaped((rows // 2, width), F32), shaped((rows // 2, width), BF)],
        (place, attended, output_weight, *out_firsts, *out_others),
    )

    def scatter_open(low, high):
        bits = xor_bits(k)
        for i, bit in enumerate(bits):
            received = swap(high, TN, bit)
            if i + 1 < len(bits):
                total = low.astype(F32) + received.astype(F32)
                half = total.shape[-2] // 2
                low, high = total[..., :half, :], total[..., half:, :].astype(BF)
        return low, received

    kept, received = scatter_open(low, high)
    residual, normed_two, stream_own = call(
        residual_kernel,
        [shaped((share, width), F32), shaped((share, width), BF), shaped((2 * share, width), BF)],
        (place, kept, received, hidden_own, gains, cot_pieces[0]),
    )

    stream = [stream_own if n == 1 else after(stream_own, moved[n // 2])]
    for r in range(1, n):
        stream.append(shift(stream[-1], 1))
    for r in range(1, n):
        unit_w.append(gather_direct(after(moved[r], attended if r == 1 else normed_two)))
    flat_units = [w for parts in unit_w for w in parts]
    carried = None
    back_kept = []
    back_received = []
    for r in range(n):
        acts = [stream[r] if r else normed_two]
        for bit in reversed(xor_bits(k)):
            acts = acts + [swap(p, TN, bit) for p in acts]
        carried, low, high = mlp_chunk(
            r, n, m, place, acts, [] if r else cot_pieces, flat_units, carried
        )
        kept, received = scatter_open(low, high)
        back_kept.append(kept)
        back_received.append(received)
    back_moved = []
    for r in range(1, n):
        part = (back_kept[r] + back_received[r].astype(F32)).astype(BF)
        back_moved.append(shift(part, -r))
    grad_residual, grad_b, gain_two_term = call(
        feed_back_kernel,
        [shaped((share, width), F32), shaped((share, width), BF), shaped((1, width), F32)],
        (place, back_kept[0], back_received[0], residual, gains, cot_pieces[0], *back_moved),
    )
    all_acts, all_cots, all_hid, all_back = carried[0], carried[1], carried[2 : 2 + m], carried[2 + m :]

    def send_part(value, j):
        return swap(value.astype(BF), CX, c_offsets[j])

    unit_terms = [[] for _ in range(n)]
    for j in reversed(range(m)):
        half = n // 2 if j else n
        parts = [None] * n
        for first in range(1, n + 1, half):
            some = unit_grads(
                place, all_acts, all_cots, all_hid[j], all_back[j],
                BF if j else F32, n, first, half,
            )
            for i, value in enumerate(some):
                parts[(first + i) % n] = value
        for i in range(n):
            r = (1 + i) % n
            if j:
                if i >= n // 2:
                    parts[r] = after(parts[r], unit_terms[1 + i - n // 2][0])
                parts[r] = send_part(parts[r], j)
            unit_terms[r].append(parts[r])
    unit_totals = []
    for r in range(n):
        total = sum(t.astype(F32) for t in unit_terms[r]).astype(BF)
        if r:
            total = shift(total, -r)
        unit_totals.append(total)
    grads = [grad_b]
    for bit in reversed(xor_bits(k)):
        grads = grads + [swap(p, TN, bit) for p in grads]
    feed_low, feed_high = feed_out(place, [after(h, grad_b) for h in all_hid], flat_units, rows, n)
    attended_grad, all_grads = call(
        lambda *refs: out_back_kernel(n, m, k, *refs),
        [shaped((rows, m * q_cols), BF), shaped((rows, width), BF)],
        (place, output_weight, *grads, *out_firsts, *out_others),
    )
    query_grad, kv_grad, *kv_sends = call(
        lambda *refs: attend_back_kernel(n, m, k, *refs),
        [shaped((rows, m * q_cols), F32), shaped((rows, wide), F32)]
        + [shaped((rows, wide), BF)] * (m - 1),
        (place, query, seg_row, seg_col, attended, attended_grad, totals, kv_own, *kv_others),
        [
            pltpu.VMEM((rows, m * rows), F32),
            pltpu.VMEM((m * rows, wide), BF),
            pltpu.VMEM((m * rows, wide), F32),
        ],
    )
    kv_received = []
    for o, sent in zip(c_offsets[1:], kv_sends):
        kv_received.append(swap(sent, CX, o))
    out_grads = call(
        lambda *refs: out_grad_kernel(n, m, *refs),
        [shaped((m * q_cols, block), BF if r == 1 % n else F32) for r in range(n)],
        (place, attended, after(all_grads, kv_grad)),
    )
    feed_bits = xor_bits(k)
    for i, bit in enumerate(feed_bits):
        if i + 1 == len(feed_bits):
            feed_high = after(feed_high, kv_grad)
        feed_received = swap(feed_high, TN, bit)
        if i + 1 < len(feed_bits):
            feed_low, feed_high = feed_add(place, after(feed_low, kv_grad), feed_received)
    feed_sum = feed_low.astype(F32) + feed_received.astype(F32)
    total = feed_sum[1 % n]
    for r in range(2, n + 1):
        moved_on = shift(total.astype(BF), 1)
        total = moved_on.astype(F32) + feed_sum[r % n]
    layer_out = (residual + total).astype(BF)[None]

    qkv_grads = call(
        lambda *refs: join_grads_kernel(m, q_cols, kv_cols, *refs),
        [shaped((rows, part_cols), BF)] * m,
        (place, query_grad, kv_grad, cosine, sine, *kv_received),
    )
    terms = [[] for _ in range(n)]
    for j in reversed(range(m)):
        parts = list(call(
            lambda *refs: qkv_grad_kernel(n, *refs),
            [shaped((block, part_cols), BF if j else F32)] * n,
            (place, normed_one, qkv_grads[j]),
        ))
        for i in range(n):
            r = (1 + i) % n
            if j:
                parts[r] = send_part(parts[r], j)
            terms[r].append(parts[r])
    total = after(out_grads[1 % n], terms[0][-1])
    for r in range(2, n + 1):
        total = shift(total.astype(BF), 1)
        total = total.astype(F32) + out_grads[r % n]
    parts = [total[j * q_cols : (j + 1) * q_cols] for j in range(m)]
    sums = list(parts)
    for o in c_offsets[1:]:
        order = [c_offsets.index(p ^ o) for p in c_offsets]
        got = swap(jnp.concatenate([parts[i] for i in order]).astype(BF), CX, o)
        sums = [s + got[j * q_cols : (j + 1) * q_cols].astype(F32) for j, s in enumerate(sums)]
    grad_output_out = join_rows([s[None] for s in sums])
    unit_parts = []
    for r in range(n):
        unit_parts.append(gather_direct(after(unit_totals[r], terms[0][-1] if r else kv_grad)))
    low, high = call(
        lambda *refs: qkv_back_kernel(n, m, *refs),
        [shaped((rows // 2, width), F32), shaped((rows // 2, width), BF)],
        (place, *qkv_grads, *flat_qkv),
    )
    kept, received = scatter_open(low, high)
    total = None
    for i in range(n):
        r = (1 + i) % n
        term = sum(t.astype(F32) for t in terms[r])
        if r:
            term = shift(term.astype(BF), -r).astype(F32)
        total = term if total is None else total + term
    qkv_parts_out = gather_direct(total.astype(BF))
    grad_query_out, grad_key_out, grad_value_out = call(
        lambda *refs: qkv_join_kernel(m, c_offsets, q_cols, kv_cols, *refs),
        [shaped((block, m * cols), F32) for cols in (q_cols, kv_cols, kv_cols)],
        (place, *qkv_parts_out),
    )
    grad_input, gain_one_term = call(
        input_back_kernel,
        [shaped((share, width), F32), shaped((1, width), F32)],
        (place, kept, received, hidden_own, gains, grad_residual),
    )
    gain_one, gain_two = gain_total(jnp.concatenate([gain_one_term, gain_two_term]))
    joined = None
    for r in range(n):
        joined = join_units(place, r, n, unit_parts[r], joined)
    grad_gate_out, grad_up_out, grad_down_out = joined
    return (
        layer_out,
        grad_input[None],
        gain_one,
        grad_query_out,
        grad_key_out,
        grad_value_out,
        grad_output_out,
        gain_two,
        grad_gate_out,
        grad_up_out,
        grad_down_out,
    )


def solution(mesh):
    placed = (
        P(SH, CX, None),
        P(SH, CX, None),
        P(SH, None),
        P(SH, CX),
        P(SH),
        P(SH, TN),
        P(SH, TN),
        P(SH, TN),
        P(TN, SH),
        P(SH),
        P(SH, TN),
        P(SH, TN),
        P(TN, SH),
    )

    return jax.shard_map(
        local,
        mesh=mesh,
        in_specs=placed,
        out_specs=(
            P(SH, (CX, TN), None),
            P(SH, (CX, TN), None),
            P(SH),
            P(SH, TN),
            P(SH, TN),
            P(SH, TN),
            P(TN, SH),
            P(SH),
            P(SH, TN),
            P(SH, TN),
            P(TN, SH),
        ),
        check_vma=False,
    )
```

time: 1750 us -> 741 us (0.42)
  waiting for transfers between devices: 1410 us -> 368 us
  Pallas kernels: 0 us -> 202 us
  matrix products: 158 us -> 0 us
  starting transfers between devices: 1.54 us -> 113 us
  blocking collectives: 97.8 us -> 0 us
    reduce_scatter x8 -> x0, waiting for transfers between devices: 519 us -> none  [the longest x2 191 us: reduce_grads(): lax.psum_scatter(terms[1].astype(jnp.bfloat16), 'shard', scatter_dimensio...]
    psum x4 -> x0, waiting for transfers between devices: 465 us -> none  [the longest x3 309 us: full_total(): return lax.psum(partial_value, 'tensor')]
    all_gather x5 -> x0, waiting for transfers between devices: 427 us -> none  [the longest x1 145 us: local(): lax.all_gather(gate_weight, 'shard', axis=0, tiled=True)]
    ppermute x0 -> x88, waiting for transfers between devices: none -> 368 us  [the longest x33 240 us: shift(): lax.ppermute(value, SH, [(i, (i + steps) % size) for i in range(size)])]
    pallas_call x0 -> x31, Pallas kernels: none -> 202 us  [the longest x15 81.3 us: call(): pl.pallas_call(kernel, out_shape=outs, in_specs=[pl.BlockSpec(memory_spac...]
    dot_general x30 -> x0, matrix products: 142 us -> none  [the longest x20 114 us: contract(): lax.dot_general(left, right, (((left_dim,), (right_dim,)), ((), ())), pre...]
    ppermute x0 -> x88, starting transfers between devices: none -> 113 us  [the longest x33 69 us: shift(): lax.ppermute(value, SH, [(i, (i + steps) % size) for i in range(size)])]
    all_gather x6 -> x0, blocking collectives: 80.9 us -> none  [the longest x1 22.4 us: local(): lax.all_gather(key_weight, 'shard', axis=0, tiled=True)]
  transfers between devices with their start and end apart: 17 -> 88, of which waited for: 15 -> 34; matrix products, arithmetic and copies ran while one was open for 8% -> 6% of each run, Pallas kernels for 0% -> 24%
where the time goes in v1:
time: 741 us; the launch traced here: 737 us
  waiting for transfers between devices  368 us (50%)
  Pallas kernels  202 us (27%)
  starting transfers between devices  113 us (15%)
  other arithmetic  30.5 us (4%)
  local copies, waits for them, and re-layouts  22 us (3%)
    ppermute x33, waiting for transfers between devices, shift(): lax.ppermute(value, SH, [(i, (i + steps) % size) for i in range(size)])  240 us
    ppermute x55, waiting for transfers between devices, swap(): return lax.ppermute(value, axis, [(i, i ^ offset) for i in range(size)])  128 us
    pallas_call x15, Pallas kernels, call(): pl.pallas_call(kernel, out_shape=outs, in_specs=[pl.BlockSpec(memory_spac...  81.3 us
    ppermute x33, starting transfers between devices, shift(): lax.ppermute(value, SH, [(i, (i + steps) % size) for i in range(size)])  69 us
    pallas_call x4, Pallas kernels, mlp_chunk(): pl.pallas_call(lambda *refs: mlp_kernel(first, r, n, k, m, refs), out_sha...  48.8 us
    ppermute x55, starting transfers between devices, swap(): return lax.ppermute(value, axis, [(i, i ^ offset) for i in range(size)])  44.3 us
    pallas_call x3, Pallas kernels, unit_grads(): pl.pallas_call(lambda *refs: unit_grad_kernel(count, *refs), out_shape=[o...  32.5 us
  transfers between devices with their start and end apart: 88, of which 34 were waited for; matrix products, arithmetic and copies ran while one was open for 6% of the time, Pallas kernels for 24%

profile of v1, /device:TPU:0, one launch (start us, length us, event | category | flops | bytes accessed | tf_op | source)
XLA Modules:
  0.0 737.2 jit_solution(11308186388227774017)
XLA Ops:
  41.7 12.2 %collective-permute-done.10.refs_3_.refs_6_ = bf16[256,512]{1,0:T(8,128)(2,1)S(1)} collective-permute-done((bf16[256,512]{1,0:T(8,128)(2,1)S(1)}, bf16[256,512]{1,0:T(8,128)(2,1)S(1)}, u32[]{:S(2)}, u32[]{:S(2)}) %collective-permute-start.10) | collective-permute-done | bytes 262176 | tf_op jit(solution)/shard_map/ppermute | solution.py:50
  76.3 17.8 %collective-permute-done.9.refs_5_.refs_8_ = bf16[512,256]{1,0:T(8,128)(2,1)S(1)} collective-permute-done((bf16[512,256]{1,0:T(8,128)(2,1)}, bf16[512,256]{1,0:T(8,128)(2,1)S(1)}, u32[]{:S(2)}, u32[]{:S(2)}) %collective-permute-start.9) | collective-permute-done | bytes 262176 | tf_op jit(solution)/shard_map/ppermute | solution.py:45
  94.8 8.9 %shard_map.223 = (bf16[512,512]{1,0:T(8,128)(2,1)}, f32[512,128]{1,0:T(8,128)}) custom-call(s32[9]{0:T(128)} %stack.60.refs_0_.place, bf16[512,512]{1,0:T(8,128)(2,1)} %get-tuple-element.144.refs_1_, s32[1,1024]{1,0:T(1,128)} %refs_2_.9, s32[1024,1]{1,0:T(8,128)} %copy.52.refs_3_, bf16[512,256]{1,0:T(8,128)(2,1)} %get-tuple-element.147.refs_4_.refs_7_, ...), custom_call_target="tpu_custom_call" | custom-call | tf_op jit(solution)/shard_map/pallas_call | solution.py:469
  122.9 11.4 %collective-permute-done.15.received = bf16[128,2048]{1,0:T(8,128)(2,1)S(1)} collective-permute-done((bf16[128,2048]{1,0:T(8,128)(2,1)S(1)}, bf16[128,2048]{1,0:T(8,128)(2,1)S(1)}, u32[]{:S(2)}, u32[]{:S(2)}) %collective-permute-start.15) | collective-permute-done | bytes 524320 | tf_op jit(solution)/shard_map/ppermute | solution.py:45
  138.5 16.6 %collective-permute-done.16.refs_13_.refs_9_.refs_7_ = bf16[768,512]{1,0:T(8,128)(2,1)S(1)} collective-permute-done((bf16[768,512]{1,0:T(8,128)(2,1)}, bf16[768,512]{1,0:T(8,128)(2,1)S(1)}, u32[]{:S(2)}, u32[]{:S(2)}) %collective-permute-start.16) | collective-permute-done | bytes 786464 | tf_op jit(solution)/shard_map/ppermute | solution.py:50
  159.6 23.6 %collective-permute-done.17.refs_1_ = bf16[256,2048]{1,0:T(8,128)(2,1)S(1)} collective-permute-done((bf16[256,2048]{1,0:T(8,128)(2,1)}, bf16[256,2048]{1,0:T(8,128)(2,1)S(1)}, u32[]{:S(2)}, u32[]{:S(2)}) %collective-permute-start.17) | collective-permute-done | bytes 1048608 | tf_op jit(solution)/shard_map/ppermute | solution.py:50
  183.2 16.8 %collective-permute-done.23.refs_11_.refs_7_.refs_5_ = bf16[768,512]{1,0:T(8,128)(2,1)S(1)} collective-permute-done((bf16[768,512]{1,0:T(8,128)(2,1)S(1)}, bf16[768,512]{1,0:T(8,128)(2,1)S(1)}, u32[]{:S(2)}, u32[]{:S(2)}) %collective-permute-start.23) | collective-permute-done | bytes 786464 | tf_op jit(solution)/shard_map/ppermute | solution.py:50
  203.0 13.7 %collective-permute-done.26.refs_15_.refs_11_.refs_9_ = bf16[768,512]{1,0:T(8,128)(2,1)S(1)} collective-permute-done((bf16[768,512]{1,0:T(8,128)(2,1)S(1)}, bf16[768,512]{1,0:T(8,128)(2,1)S(1)}, u32[]{:S(2)}, u32[]{:S(2)}) %collective-permute-start.26) | collective-permute-done | bytes 786464 | tf_op jit(solution)/shard_map/ppermute | solution.py:50
  220.4 17.8 %collective-permute-done.18.refs_1_ = bf16[256,2048]{1,0:T(8,128)(2,1)S(1)} collective-permute-done((bf16[256,2048]{1,0:T(8,128)(2,1)S(1)}, bf16[256,2048]{1,0:T(8,128)(2,1)S(1)}, u32[]{:S(2)}, u32[]{:S(2)}) %collective-permute-start.18) | collective-permute-done | bytes 1048608 | tf_op jit(solution)/shard_map/ppermute | solution.py:50
  239.7 13.3 %collective-permute-done.25.refs_14_.refs_10_.refs_8_ = bf16[768,512]{1,0:T(8,128)(2,1)S(1)} collective-permute-done((bf16[768,512]{1,0:T(8,128)(2,1)S(1)}, bf16[768,512]{1,0:T(8,128)(2,1)S(1)}, u32[]{:S(2)}, u32[]{:S(2)}) %collective-permute-start.25) | collective-permute-done | bytes 786464 | tf_op jit(solution)/shard_map/ppermute | solution.py:45
  253.5 10.4 %collective-permute-done.19.refs_1_ = bf16[256,2048]{1,0:T(8,128)(2,1)S(1)} collective-permute-done((bf16[256,2048]{1,0:T(8,128)(2,1)S(1)}, bf16[256,2048]{1,0:T(8,128)(2,1)S(1)}, u32[]{:S(2)}, u32[]{:S(2)}) %collective-permute-start.19) | collective-permute-done | bytes 1048608 | tf_op jit(solution)/shard_map/ppermute | solution.py:50
  267.6 12.0 %mc.4 = (bf16[2048,2048]{1,0:T(8,128)(2,1)}, bf16[2048,2048]{1,0:T(8,128)(2,1)}, bf16[2048,256]{1,0:T(8,128)(2,1)}, bf16[2048,256]{1,0:T(8,128)(2,1)}, bf16[2048...) custom-call(s32[9]{0:T(128)} %stack.60.refs_0_.place, ...), custom_call_target="tpu_custom_call" | custom-call | tf_op jit(solution)/shard_map/mc/pallas_call | solution.py:204
  280.3 9.1 %collective-permute-done.20.refs_2_ = bf16[256,2048]{1,0:T(8,128)(2,1)} collective-permute-done((bf16[256,2048]{1,0:T(8,128)(2,1)S(1)}, bf16[256,2048]{1,0:T(8,128)(2,1)}, u32[]{:S(2)}, u32[]{:S(2)}) %collective-permute-start.20) | collective-permute-done | bytes 1048608 | tf_op jit(solution)/shard_map/ppermute | solution.py:45
  289.4 12.0 %mc.5 = (bf16[2048,2048]{1,0:T(8,128)(2,1)}, bf16[2048,2048]{1,0:T(8,128)(2,1)}, bf16[2048,256]{1,0:T(8,128)(2,1)}, bf16[2048,256]{1,0:T(8,128)(2,1)}, bf16[2048...) custom-call(s32[9]{0:T(128)} %stack.60.refs_0_.place, ...), custom_call_target="tpu_custom_call", output_to_operand_aliasing={{0}: (13, {}), {1}: (14, {}), {2}: (15, {}), {3}: (16, {}),... | custom-call | tf_op jit(solution)/shard_map/mc/pallas_call | solution.py:204
  302.1 12.6 %mc.6 = (bf16[2048,2048]{1,0:T(8,128)(2,1)}, bf16[2048,2048]{1,0:T(8,128)(2,1)}, bf16[2048,256]{1,0:T(8,128)(2,1)}, bf16[2048,256]{1,0:T(8,128)(2,1)}, bf16[2048...) custom-call(s32[9]{0:T(128)} %stack.60.refs_0_.place, ...), custom_call_target="tpu_custom_call", output_to_operand_aliasing={{0}: (13, {}), {1}: (14, {}), {2}: (15, {}), {3}: (16, {}),... | custom-call | tf_op jit(solution)/shard_map/mc/pallas_call | solution.py:204
  320.1 12.1 %mc.7 = (bf16[2048,2048]{1,0:T(8,128)(2,1)}, bf16[2048,2048]{1,0:T(8,128)(2,1)}, bf16[2048,256]{1,0:T(8,128)(2,1)}, bf16[2048,256]{1,0:T(8,128)(2,1)}, bf16[2048...) custom-call(s32[9]{0:T(128)} %stack.60.refs_0_.place, ...), custom_call_target="tpu_custom_call", output_to_operand_aliasing={{0}: (13, {}), {1}: (14, {}), {2}: (15, {}), {3}: (16, {}),... | custom-call | tf_op jit(solution)/shard_map/mc/pallas_call | solution.py:204
  339.2 9.8 %collective-permute-done.40 = bf16[128,2048]{1,0:T(8,128)(2,1)S(1)} collective-permute-done((bf16[128,2048]{1,0:T(8,128)(2,1)S(1)}, bf16[128,2048]{1,0:T(8,128)(2,1)S(1)}, u32[]{:S(2)}, u32[]{:S(2)}) %collective-permute-start.40) | collective-permute-done | bytes 524320 | tf_op jit(solution)/shard_map/ppermute | solution.py:45
  349.2 20.1 %collective-permute-start.41 = (bf16[128,2048]{1,0:T(8,128)(2,1)S(1)}, bf16[128,2048]{1,0:T(8,128)(2,1)S(1)}, u32[]{:S(2)}, u32[]{:S(2)}) collective-permute-start(bf16[128,2048]{1,0:T(8,128)(2,1)S(1)} %fusion.9), channel_id=1, source_target_pairs={{0,24},{8,0},{16,8},{24,16},{1,25},{9,1},{17,9},{25,17},{2,26},{10... | collective-permute-start | bytes 1572872 | tf_op jit(solution)/shard_map/ppermute | solution.py:50
  369.4 9.2 %collective-permute-start.44 = (bf16[128,2048]{1,0:T(8,128)(2,1)S(1)}, bf16[128,2048]{1,0:T(8,128)(2,1)S(1)}, u32[]{:S(2)}, u32[]{:S(2)}) collective-permute-start(bf16[128,2048]{1,0:T(8,128)(2,1)S(1)} %fusion.8), channel_id=1, source_target_pairs={{0,16},{8,24},{16,0},{24,8},{1,17},{9,25},{17,1},{25,9},{2,18},{10... | collective-permute-start | bytes 1572872 | tf_op jit(solution)/shard_map/ppermute | solution.py:50
  382.4 29.6 %collective-permute-done.44.refs_1_ = bf16[128,2048]{1,0:T(8,128)(2,1)S(1)} collective-permute-done((bf16[128,2048]{1,0:T(8,128)(2,1)S(1)}, bf16[128,2048]{1,0:T(8,128)(2,1)S(1)}, u32[]{:S(2)}, u32[]{:S(2)}) %collective-permute-start.44) | collective-permute-done | bytes 524320 | tf_op jit(solution)/shard_map/ppermute | solution.py:50
  417.4 9.5 %fo.1 = (bf16[4,256,2048]{2,1,0:T(8,128)(2,1)}, bf16[4,256,2048]{2,1,0:T(8,128)(2,1)}) custom-call(s32[9]{0:T(128)} %stack.60.refs_0_.place, bf16[4,512,256]{2,1,0:T(8,128)(2,1)} %bitcast.68, bf16[4,512,256]{2,1,0:T(8,128)(2,1)} %bitcast.67, bf16[768,512]{1,0:T(8,128)(2,1)} %get-tuple-element.161.refs_9_.refs_5_.refs_3_, ...), custom_call_target="tpu_custom_call" | custom-call | tf_op jit(solution)/shard_map/fo/pallas_call | solution.py:246
  426.9 9.0 %shard_map.237 = (bf16[768,512]{1,0:T(8,128)(2,1)}, bf16[768,512]{1,0:T(8,128)(2,1)}) custom-call(s32[9]{0:T(128)} %stack.60.refs_0_.place, bf16[2048,2048]{1,0:T(8,128)(2,1)} %get-tuple-element.241.refs_1_, bf16[2048,2048]{1,0:T(8,128)(2,1)} %get-tuple-element.242.refs_2_, bf16[2048,256]{1,0:T(8,128)(2,1)} %get-tuple-element.203.refs_3_, ...), custom_call_target="tpu_custom_call" | custom-call | tf_op jit(solution)/shard_map/pallas_call | solution.py:342
  438.5 8.9 %shard_map.236 = (bf16[768,512]{1,0:T(8,128)(2,1)}, bf16[768,512]{1,0:T(8,128)(2,1)}) custom-call(s32[9]{0:T(128)} %stack.60.refs_0_.place, bf16[2048,2048]{1,0:T(8,128)(2,1)} %get-tuple-element.241.refs_1_, bf16[2048,2048]{1,0:T(8,128)(2,1)} %get-tuple-element.242.refs_2_, bf16[2048,256]{1,0:T(8,128)(2,1)} %get-tuple-element.203.refs_3_, ...), custom_call_target="tpu_custom_call" | custom-call | tf_op jit(solution)/shard_map/pallas_call | solution.py:342
  447.3 9.2 %collective-permute-done.77 = bf16[768,512]{1,0:T(8,128)(2,1)S(1)} collective-permute-done((bf16[768,512]{1,0:T(8,128)(2,1)}, bf16[768,512]{1,0:T(8,128)(2,1)S(1)}, u32[]{:S(2)}, u32[]{:S(2)}) %collective-permute-start.77) | collective-permute-done | bytes 786464 | tf_op jit(solution)/shard_map/ppermute | solution.py:45
  458.0 14.6 %shard_map.238 = (f32[768,512]{1,0:T(8,128)}, f32[768,512]{1,0:T(8,128)}, f32[768,512]{1,0:T(8,128)}, f32[768,512]{1,0:T(8,128)}) custom-call(s32[9]{0:T(128)} %stack.60.refs_0_.place, bf16[2048,2048]{1,0:T(8,128)(2,1)} %get-tuple-element.241.refs_1_, bf16[2048,2048]{1,0:T(8,128)(2,1)} %get-tuple-element.242.refs_2_, ...), custom_call_target="tpu_custom_call" | custom-call | tf_op jit(solution)/shard_map/pallas_call | solution.py:342
  487.6 17.4 %shard_map.228 = (f32[512,512]{1,0:T(8,128)}, f32[512,256]{1,0:T(8,128)}, bf16[512,256]{1,0:T(8,128)(2,1)}) custom-call(s32[9]{0:T(128)} %stack.60.refs_0_.place, bf16[512,512]{1,0:T(8,128)(2,1)} %get-tuple-element.144.refs_1_, s32[1,1024]{1,0:T(1,128)} %refs_2_.9, s32[1024,1]{1,0:T(8,128)} %copy.52.refs_3_, ...), custom_call_target="tpu_custom_call" | custom-call | tf_op jit(solution)/shard_map/pallas_call | solution.py:469
  524.8 26.3 %collective-permute-done.82.refs_1_ = bf16[768,512]{1,0:T(8,128)(2,1)} collective-permute-done((bf16[768,512]{1,0:T(8,128)(2,1)}, bf16[768,512]{1,0:T(8,128)(2,1)}, u32[]{:S(2)}, u32[]{:S(2)}) %collective-permute-start.82) | collective-permute-done | bytes 786464 | tf_op jit(solution)/shard_map/ppermute | solution.py:50
  596.1 21.0 %collective-permute-done.68 = bf16[512,384]{1,0:T(8,128)(2,1)} collective-permute-done((bf16[512,384]{1,0:T(8,128)(2,1)}, bf16[512,384]{1,0:T(8,128)(2,1)}, u32[]{:S(2)}, u32[]{:S(2)}) %collective-permute-start.68) | collective-permute-done | bytes 393248 | tf_op jit(solution)/shard_map/ppermute | solution.py:50
  622.7 14.9 %collective-permute-done.85.refs_2_ = bf16[768,512]{1,0:T(8,128)(2,1)S(1)} collective-permute-done((bf16[768,512]{1,0:T(8,128)(2,1)S(1)}, bf16[768,512]{1,0:T(8,128)(2,1)S(1)}, u32[]{:S(2)}, u32[]{:S(2)}) %collective-permute-start.85) | collective-permute-done | bytes 786464 | tf_op jit(solution)/shard_map/ppermute | solution.py:45
  640.6 13.9 %collective-permute-done.83.refs_2_ = bf16[768,512]{1,0:T(8,128)(2,1)} collective-permute-done((bf16[768,512]{1,0:T(8,128)(2,1)}, bf16[768,512]{1,0:T(8,128)(2,1)}, u32[]{:S(2)}, u32[]{:S(2)}) %collective-permute-start.83) | collective-permute-done | bytes 786464 | tf_op jit(solution)/shard_map/ppermute | solution.py:45
  691.1 14.9 %collective-permute-done.53 = bf16[128,2048]{1,0:T(8,128)(2,1)S(1)} collective-permute-done((bf16[128,2048]{1,0:T(8,128)(2,1)S(1)}, bf16[128,2048]{1,0:T(8,128)(2,1)S(1)}, u32[]{:S(2)}, u32[]{:S(2)}) %collective-permute-start.53) | collective-permute-done | bytes 524320 | tf_op jit(solution)/shard_map/ppermute | solution.py:50
  725.9 10.1 %collective-permute-done.55 = bf16[128,2048]{1,0:T(8,128)(2,1)S(1)} collective-permute-done((bf16[128,2048]{1,0:T(8,128)(2,1)S(1)}, bf16[128,2048]{1,0:T(8,128)(2,1)S(1)}, u32[]{:S(2)}, u32[]{:S(2)}) %collective-permute-start.55) | collective-permute-done | bytes 524320 | tf_op jit(solution)/shard_map/ppermute | solution.py:50
  (371 shorter events, 276.5 us)
Async XLA Ops:
  114.7 40.4 %collective-permute-start.16 = (bf16[768,512]{1,0:T(8,128)(2,1)}, bf16[768,512]{1,0:T(8,128)(2,1)S(1)}, u32[]{:S(2)}, u32[]{:S(2)}) collective-permute-start(bf16[768,512]{1,0:T(8,128)(2,1)} %get-tuple-element.159), channel_id=1, source_target_pairs={{0,16},{8,24},{16,0},{24,8},{1,17},{9,25},{17,1},{25,9},{2,18},{10... | collective-permute-start | bytes 2359304 | tf_op jit(solution)/shard_map/ppermute | solution.py:50
  155.8 44.3 %collective-permute-start.23 = (bf16[768,512]{1,0:T(8,128)(2,1)S(1)}, bf16[768,512]{1,0:T(8,128)(2,1)S(1)}, u32[]{:S(2)}, u32[]{:S(2)}) collective-permute-start(bf16[768,512]{1,0:T(8,128)(2,1)S(1)} %copy-done.63), channel_id=1, source_target_pairs={{0,8},{8,16},{16,24},{24,0},{1,9},{9,17},{17,25},{25,1},{2,10},{10... | collective-permute-start | bytes 2359304 | tf_op jit(solution)/shard_map/ppermute | solution.py:50
  155.8 61.0 %collective-permute-start.26 = (bf16[768,512]{1,0:T(8,128)(2,1)S(1)}, bf16[768,512]{1,0:T(8,128)(2,1)S(1)}, u32[]{:S(2)}, u32[]{:S(2)}) collective-permute-start(bf16[768,512]{1,0:T(8,128)(2,1)S(1)} %copy-done.62), channel_id=1, source_target_pairs={{0,24},{8,0},{16,8},{24,16},{1,25},{9,1},{17,9},{25,17},{2,26},{10... | collective-permute-start | bytes 2359304 | tf_op jit(solution)/shard_map/ppermute | solution.py:50
  183.2 54.9 %collective-permute-start.18 = (bf16[256,2048]{1,0:T(8,128)(2,1)S(1)}, bf16[256,2048]{1,0:T(8,128)(2,1)S(1)}, u32[]{:S(2)}, u32[]{:S(2)}) collective-permute-start(bf16[256,2048]{1,0:T(8,128)(2,1)S(1)} %collective-permute-done.17.refs_1_), channel_id=1, source_target_pairs={{0,8},{8,16},{16,24},{24,0},{1,9},{9,17},{17,25},{25,1},{2,10},{10... | collective-permute-start | bytes 3145736 | tf_op jit(solution)/shard_map/ppermute | solution.py:50
  218.3 34.7 %collective-permute-start.25 = (bf16[768,512]{1,0:T(8,128)(2,1)S(1)}, bf16[768,512]{1,0:T(8,128)(2,1)S(1)}, u32[]{:S(2)}, u32[]{:S(2)}) collective-permute-start(bf16[768,512]{1,0:T(8,128)(2,1)S(1)} %collective-permute-done.16.refs_13_.refs_9_.refs_7_), channel_id=1, source_target_pairs={{0,4},{4,0},{1,5},{5,1},{2,6},{6,2},{3,7},{7,3},{8,12},{12,8},{9,1... | collective-permute-start | bytes 2359304 | tf_op jit(solution)/shard_map/ppermute | solution.py:45
  218.8 34.2 %collective-permute-start.31 = (bf16[256,2048]{1,0:T(8,128)(2,1)S(1)}, bf16[256,2048]{1,0:T(8,128)(2,1)}, u32[]{:S(2)}, u32[]{:S(2)}) collective-permute-start(bf16[256,2048]{1,0:T(8,128)(2,1)S(1)} %collective-permute-done.17.refs_1_), channel_id=1, source_target_pairs={{0,2},{1,3},{2,0},{3,1},{4,6},{5,7},{6,4},{7,5},{8,10},{9,11},{10,... | collective-permute-start | bytes 3145736 | tf_op jit(solution)/shard_map/ppermute | solution.py:45
  239.7 39.9 %collective-permute-start.32 = (bf16[256,2048]{1,0:T(8,128)(2,1)S(1)}, bf16[256,2048]{1,0:T(8,128)(2,1)}, u32[]{:S(2)}, u32[]{:S(2)}) collective-permute-start(bf16[256,2048]{1,0:T(8,128)(2,1)S(1)} %collective-permute-done.17.refs_1_), channel_id=1, source_target_pairs={{0,1},{1,0},{2,3},{3,2},{4,5},{5,4},{6,7},{7,6},{8,9},{9,8},{10,11... | collective-permute-start | bytes 3145736 | tf_op jit(solution)/shard_map/ppermute | solution.py:45
  265.4 36.1 %collective-permute-start.29 = (bf16[256,2048]{1,0:T(8,128)(2,1)S(1)}, bf16[256,2048]{1,0:T(8,128)(2,1)}, u32[]{:S(2)}, u32[]{:S(2)}) collective-permute-start(bf16[256,2048]{1,0:T(8,128)(2,1)S(1)} %collective-permute-done.18.refs_1_), channel_id=1, source_target_pairs={{0,1},{1,0},{2,3},{3,2},{4,5},{5,4},{6,7},{7,6},{8,9},{9,8},{10,11... | collective-permute-start | bytes 3145736 | tf_op jit(solution)/shard_map/ppermute | solution.py:45
  267.5 34.6 %collective-permute-start.30 = (bf16[256,2048]{1,0:T(8,128)(2,1)}, bf16[256,2048]{1,0:T(8,128)(2,1)}, u32[]{:S(2)}, u32[]{:S(2)}) collective-permute-start(bf16[256,2048]{1,0:T(8,128)(2,1)} %collective-permute-done.28.refs_2_), channel_id=1, source_target_pairs={{0,1},{1,0},{2,3},{3,2},{4,5},{5,4},{6,7},{7,6},{8,9},{9,8},{10,11... | collective-permute-start | bytes 3145736 | tf_op jit(solution)/shard_map/ppermute | solution.py:45
  279.6 35.2 %collective-permute-start.37 = (bf16[256,2048]{1,0:T(8,128)(2,1)}, bf16[256,2048]{1,0:T(8,128)(2,1)}, u32[]{:S(2)}, u32[]{:S(2)}) collective-permute-start(bf16[256,2048]{1,0:T(8,128)(2,1)} %get-tuple-element.193), channel_id=1, source_target_pairs={{0,1},{1,0},{2,3},{3,2},{4,5},{5,4},{6,7},{7,6},{8,9},{9,8},{10,11... | collective-permute-start | bytes 3145736 | tf_op jit(solution)/shard_map/ppermute | solution.py:45
  280.2 38.6 %collective-permute-start.21 = (bf16[256,2048]{1,0:T(8,128)(2,1)S(1)}, bf16[256,2048]{1,0:T(8,128)(2,1)S(1)}, u32[]{:S(2)}, u32[]{:S(2)}) collective-permute-start(bf16[256,2048]{1,0:T(8,128)(2,1)S(1)} %collective-permute-done.19.refs_1_), channel_id=1, source_target_pairs={{0,1},{1,0},{2,3},{3,2},{4,5},{5,4},{6,7},{7,6},{8,9},{9,8},{10,11... | collective-permute-start | bytes 3145736 | tf_op jit(solution)/shard_map/ppermute | solution.py:45
  317.3 65.1 %collective-permute-start.38 = (bf16[128,2048]{1,0:T(8,128)(2,1)}, bf16[128,2048]{1,0:T(8,128)(2,1)S(1)}, u32[]{:S(2)}, u32[]{:S(2)}) collective-permute-start(bf16[128,2048]{1,0:T(8,128)(2,1)} %slice.154), channel_id=1, source_target_pairs={{0,2},{1,3},{2,0},{3,1},{4,6},{5,7},{6,4},{7,5},{8,10},{9,11},{10,... | collective-permute-start | bytes 1572872 | tf_op jit(solution)/shard_map/ppermute | solution.py:45
  338.6 40.0 %collective-permute-start.46 = (bf16[128,2048]{1,0:T(8,128)(2,1)S(1)}, bf16[128,2048]{1,0:T(8,128)(2,1)S(1)}, u32[]{:S(2)}, u32[]{:S(2)}) collective-permute-start(bf16[128,2048]{1,0:T(8,128)(2,1)S(1)} %slice.151), channel_id=1, source_target_pairs={{0,2},{1,3},{2,0},{3,1},{4,6},{5,7},{6,4},{7,5},{8,10},{9,11},{10,... | collective-permute-start | bytes 1572872 | tf_op jit(solution)/shard_map/ppermute | solution.py:45
  369.4 42.6 %collective-permute-start.44 = (bf16[128,2048]{1,0:T(8,128)(2,1)S(1)}, bf16[128,2048]{1,0:T(8,128)(2,1)S(1)}, u32[]{:S(2)}, u32[]{:S(2)}) collective-permute-start(bf16[128,2048]{1,0:T(8,128)(2,1)S(1)} %fusion.8), channel_id=1, source_target_pairs={{0,16},{8,24},{16,0},{24,8},{1,17},{9,25},{17,1},{25,9},{2,18},{10... | collective-permute-start | bytes 1572872 | tf_op jit(solution)/shard_map/ppermute | solution.py:50
  426.9 159.8 %collective-permute-start.51 = (bf16[4,256,2048]{2,1,0:T(8,128)(2,1)}, bf16[4,256,2048]{2,1,0:T(8,128)(2,1)S(1)}, u32[]{:S(2)}, u32[]{:S(2)}) collective-permute-start(bf16[4,256,2048]{2,1,0:T(8,128)(2,1)} %get-tuple-element.209), channel_id=1, source_target_pairs={{0,1},{1,0},{2,3},{3,2},{4,5},{5,4},{6,7},{7,6},{8,9},{9,8},{10,11... | collective-permute-start | bytes 12582920 | tf_op jit(solution)/shard_map/ppermute | solution.py:45
  437.4 36.0 %collective-permute-start.81 = (bf16[768,512]{1,0:T(8,128)(2,1)}, bf16[768,512]{1,0:T(8,128)(2,1)S(1)}, u32[]{:S(2)}, u32[]{:S(2)}) collective-permute-start(bf16[768,512]{1,0:T(8,128)(2,1)} %get-tuple-element.250), channel_id=1, source_target_pairs={{0,4},{4,0},{1,5},{5,1},{2,6},{6,2},{3,7},{7,3},{8,12},{12,8},{9,1... | collective-permute-start | bytes 2359304 | tf_op jit(solution)/shard_map/ppermute | solution.py:45
  437.9 37.0 %collective-permute-start.48 = (bf16[128,2048]{1,0:T(8,128)(2,1)S(1)}, bf16[128,2048]{1,0:T(8,128)(2,1)}, u32[]{:S(2)}, u32[]{:S(2)}) collective-permute-start(bf16[128,2048]{1,0:T(8,128)(2,1)S(1)} %copy-done.46), channel_id=1, source_target_pairs={{0,2},{1,3},{2,0},{3,1},{4,6},{5,7},{6,4},{7,5},{8,10},{9,11},{10,... | collective-permute-start | bytes 1572872 | tf_op jit(solution)/shard_map/ppermute | solution.py:45
  438.5 39.0 %collective-permute-start.49 = (bf16[128,2048]{1,0:T(8,128)(2,1)S(1)}, bf16[128,2048]{1,0:T(8,128)(2,1)}, u32[]{:S(2)}, u32[]{:S(2)}) collective-permute-start(bf16[128,2048]{1,0:T(8,128)(2,1)S(1)} %copy-done.46), channel_id=1, source_target_pairs={{0,1},{1,0},{2,3},{3,2},{4,5},{5,4},{6,7},{7,6},{8,9},{9,8},{10,11... | collective-permute-start | bytes 1572872 | tf_op jit(solution)/shard_map/ppermute | solution.py:45
  456.5 48.6 %collective-permute-start.78 = (bf16[768,512]{1,0:T(8,128)(2,1)}, bf16[768,512]{1,0:T(8,128)(2,1)S(1)}, u32[]{:S(2)}, u32[]{:S(2)}) collective-permute-start(bf16[768,512]{1,0:T(8,128)(2,1)} %get-tuple-element.246), channel_id=1, source_target_pairs={{0,4},{4,0},{1,5},{5,1},{2,6},{6,2},{3,7},{7,3},{8,12},{12,8},{9,1... | collective-permute-start | bytes 2359304 | tf_op jit(solution)/shard_map/ppermute | solution.py:45
  473.4 49.4 %collective-permute-start.86 = (bf16[768,512]{1,0:T(8,128)(2,1)}, bf16[768,512]{1,0:T(8,128)(2,1)}, u32[]{:S(2)}, u32[]{:S(2)}) collective-permute-start(bf16[768,512]{1,0:T(8,128)(2,1)} %get-tuple-element.256), channel_id=1, source_target_pairs={{0,4},{4,0},{1,5},{5,1},{2,6},{6,2},{3,7},{7,3},{8,12},{12,8},{9,1... | collective-permute-start | bytes 2359304 | tf_op jit(solution)/shard_map/ppermute | solution.py:45
  477.4 46.1 %collective-permute-start.84 = (bf16[768,512]{1,0:T(8,128)(2,1)}, bf16[768,512]{1,0:T(8,128)(2,1)S(1)}, u32[]{:S(2)}, u32[]{:S(2)}) collective-permute-start(bf16[768,512]{1,0:T(8,128)(2,1)} %add_convert_fusion.1), channel_id=1, source_target_pairs={{0,24},{8,0},{16,8},{24,16},{1,25},{9,1},{17,9},{25,17},{2,26},{10... | collective-permute-start | bytes 2359304 | tf_op jit(solution)/shard_map/ppermute | solution.py:50
  482.2 68.9 %collective-permute-start.82 = (bf16[768,512]{1,0:T(8,128)(2,1)}, bf16[768,512]{1,0:T(8,128)(2,1)}, u32[]{:S(2)}, u32[]{:S(2)}) collective-permute-start(bf16[768,512]{1,0:T(8,128)(2,1)} %add_convert_fusion.2), channel_id=1, source_target_pairs={{0,16},{8,24},{16,0},{24,8},{1,17},{9,25},{17,1},{25,9},{2,18},{10... | collective-permute-start | bytes 2359304 | tf_op jit(solution)/shard_map/ppermute | solution.py:50
  513.8 54.0 %collective-permute-start.79 = (bf16[768,512]{1,0:T(8,128)(2,1)}, bf16[768,512]{1,0:T(8,128)(2,1)}, u32[]{:S(2)}, u32[]{:S(2)}) collective-permute-start(bf16[768,512]{1,0:T(8,128)(2,1)} %add_convert_fusion.3), channel_id=1, source_target_pairs={{0,8},{8,16},{16,24},{24,0},{1,9},{9,17},{17,25},{25,1},{2,10},{10... | collective-permute-start | bytes 2359304 | tf_op jit(solution)/shard_map/ppermute | solution.py:50
  522.7 45.1 %collective-permute-start.65 = (bf16[512,384]{1,0:T(8,128)(2,1)}, bf16[512,384]{1,0:T(8,128)(2,1)}, u32[]{:S(2)}, u32[]{:S(2)}) collective-permute-start(bf16[512,384]{1,0:T(8,128)(2,1)} %get-tuple-element.223), channel_id=1, source_target_pairs={{0,4},{4,0},{1,5},{5,1},{2,6},{6,2},{3,7},{7,3},{8,12},{12,8},{9,1... | collective-permute-start | bytes 1179656 | tf_op jit(solution)/shard_map/ppermute | solution.py:45
  523.5 47.8 %collective-permute-start.67 = (bf16[512,384]{1,0:T(8,128)(2,1)}, bf16[512,384]{1,0:T(8,128)(2,1)}, u32[]{:S(2)}, u32[]{:S(2)}) collective-permute-start(bf16[512,384]{1,0:T(8,128)(2,1)} %get-tuple-element.225), channel_id=1, source_target_pairs={{0,4},{4,0},{1,5},{5,1},{2,6},{6,2},{3,7},{7,3},{8,12},{12,8},{9,1... | collective-permute-start | bytes 1179656 | tf_op jit(solution)/shard_map/ppermute | solution.py:45
  571.3 51.0 %collective-permute-start.57 = (bf16[256,2048]{1,0:T(8,128)(2,1)}, bf16[256,2048]{1,0:T(8,128)(2,1)S(1)}, u32[]{:S(2)}, u32[]{:S(2)}) collective-permute-start(bf16[256,2048]{1,0:T(8,128)(2,1)} %get-tuple-element.218), channel_id=1, source_target_pairs={{0,1},{1,0},{2,3},{3,2},{4,5},{5,4},{6,7},{7,6},{8,9},{9,8},{10,11... | collective-permute-start | bytes 3145736 | tf_op jit(solution)/shard_map/ppermute | solution.py:45
  578.8 41.9 %collective-permute-start.87 = (bf16[768,512]{1,0:T(8,128)(2,1)S(1)}, bf16[768,512]{1,0:T(8,128)(2,1)}, u32[]{:S(2)}, u32[]{:S(2)}) collective-permute-start(bf16[768,512]{1,0:T(8,128)(2,1)S(1)} %add_convert_fusion.refs_1_), channel_id=1, source_target_pairs={{0,4},{4,0},{1,5},{5,1},{2,6},{6,2},{3,7},{7,3},{8,12},{12,8},{9,1... | collective-permute-start | bytes 2359304 | tf_op jit(solution)/shard_map/ppermute | solution.py:45
  595.3 90.7 %collective-permute-start.52 = (bf16[4,128,2048]{2,1,0:T(8,128)(2,1)}, bf16[4,128,2048]{2,1,0:T(8,128)(2,1)}, u32[]{:S(2)}, u32[]{:S(2)}) collective-permute-start(bf16[4,128,2048]{2,1,0:T(8,128)(2,1)} %get-tuple-element.212), channel_id=1, source_target_pairs={{0,2},{1,3},{2,0},{3,1},{4,6},{5,7},{6,4},{7,5},{8,10},{9,11},{10,... | collective-permute-start | bytes 6291464 | tf_op jit(solution)/shard_map/ppermute | solution.py:45
  618.7 35.8 %collective-permute-start.83 = (bf16[768,512]{1,0:T(8,128)(2,1)}, bf16[768,512]{1,0:T(8,128)(2,1)}, u32[]{:S(2)}, u32[]{:S(2)}) collective-permute-start(bf16[768,512]{1,0:T(8,128)(2,1)} %collective-permute-done.82.refs_1_), channel_id=1, source_target_pairs={{0,4},{4,0},{1,5},{5,1},{2,6},{6,2},{3,7},{7,3},{8,12},{12,8},{9,1... | collective-permute-start | bytes 2359304 | tf_op jit(solution)/shard_map/ppermute | solution.py:45
  620.7 50.7 %collective-permute-start.80 = (bf16[768,512]{1,0:T(8,128)(2,1)}, bf16[768,512]{1,0:T(8,128)(2,1)}, u32[]{:S(2)}, u32[]{:S(2)}) collective-permute-start(bf16[768,512]{1,0:T(8,128)(2,1)} %collective-permute-done.79.refs_1_), channel_id=1, source_target_pairs={{0,4},{4,0},{1,5},{5,1},{2,6},{6,2},{3,7},{7,3},{8,12},{12,8},{9,1... | collective-permute-start | bytes 2359304 | tf_op jit(solution)/shard_map/ppermute | solution.py:45
  637.6 41.3 %collective-permute-start.72 = (bf16[512,384]{1,0:T(8,128)(2,1)S(1)}, bf16[512,384]{1,0:T(8,128)(2,1)}, u32[]{:S(2)}, u32[]{:S(2)}) collective-permute-start(bf16[512,384]{1,0:T(8,128)(2,1)S(1)} %add_convert_fusion.6.refs_1_), channel_id=1, source_target_pairs={{0,4},{4,0},{1,5},{5,1},{2,6},{6,2},{3,7},{7,3},{8,12},{12,8},{9,1... | collective-permute-start | bytes 1179656 | tf_op jit(solution)/shard_map/ppermute | solution.py:45
  639.1 42.3 %collective-permute-start.58 = (bf16[128,2048]{1,0:T(8,128)(2,1)S(1)}, bf16[128,2048]{1,0:T(8,128)(2,1)}, u32[]{:S(2)}, u32[]{:S(2)}) collective-permute-start(bf16[128,2048]{1,0:T(8,128)(2,1)S(1)} %slice.150), channel_id=1, source_target_pairs={{0,2},{1,3},{2,0},{3,1},{4,6},{5,7},{6,4},{7,5},{8,10},{9,11},{10,... | collective-permute-start | bytes 1572872 | tf_op jit(solution)/shard_map/ppermute | solution.py:45
  (120 other events, 2319.1 us)

commit v2 on v1

--- a/solution.py
+++ b/solution.py
@@ -56,6 +56,16 @@
 
 def gather_direct(value):
     return [value] + [swap(value, CX, o) for o in xor_offsets(lax.axis_size(CX))[1:]]
+
+
+def shard_sum(terms):
+    left = dict(enumerate(terms))
+    for bit in xor_bits(len(terms)):
+        kept = [o for o in left if not o & bit]
+        sent = [left[o | bit].astype(BF) for o in kept]
+        got = swap(jnp.stack(sent) if len(sent) > 1 else sent[0][None], SH, bit)
+        left = {o: left[o].astype(F32) + got[i].astype(F32) for i, o in enumerate(kept)}
+    return left[0]
 
 
 def turn_blocks(value, dim):
@@ -263,20 +273,20 @@
     sent[...] = total[half:].astype(BF)
 
 
-def feed_add(place, low, received):
+def feed_add(places, low, received):
     n, rows, width = low.shape
     half = rows // 2
-    part = pl.BlockSpec((None, half, width), lambda i: (i, 0, 0))
-    full = pl.BlockSpec((1, rows, width), lambda i: (i, 0, 0))
+    part = pl.BlockSpec((None, half, width), lambda i, places: (i, 0, 0))
+    full = pl.BlockSpec((1, rows, width), lambda i, places: (places[i], 0, 0))
     return pl.pallas_call(
         feed_add_kernel,
-        grid=(n,),
         out_shape=[jax.ShapeDtypeStruct((n, half, width), t) for t in (F32, BF)],
-        in_specs=[pl.BlockSpec(memory_space=pltpu.SMEM), full, full],
-        out_specs=[part, part],
+        grid_spec=pltpu.PrefetchScalarGridSpec(
+            num_scalar_prefetch=1, grid=(n,), in_specs=[full, full], out_specs=[part, part]
+        ),
         compiler_params=params(),
         name="fa",
-    )(place, low, received)
+    )(places, low, received)
 
 
 def spread_kernel(n, m, place, gate, up, down, *outs):
@@ -658,11 +668,13 @@
         attended_grad[:, j * part : (j + 1) * part] = total.astype(BF)
 
 
-def out_grad_kernel(n, m, place, attended, grads, *outs):
+def out_grad_kernel(n, m, k, place, attended, grads, *outs):
     part, block = attended.shape[1] // m, grads.shape[1] // n
     for j in reversed(range(m)):
         for r in range(n):
-            total = contract(attended[:, j * part : (j + 1) * part], grads[:, at(place, 1 + r, block)], 0, 0)
+            total = contract(
+                attended[:, j * part : (j + 1) * part], grads[:, at(place, 1 + n + k + r, block)], 0, 0
+            )
             outs[r][j * part : (j + 1) * part, :] = total.astype(outs[r].dtype)
 
 
@@ -721,11 +733,11 @@
         outs[j][:, q_cols + kv_cols :] = values[:, j * kv_cols : (j + 1) * kv_cols]
 
 
-def qkv_grad_kernel(n, place, normed, grads, *outs):
+def qkv_grad_kernel(n, k, place, normed, grads, *outs):
     block = normed.shape[1] // n
     for i in range(n):
         r = (1 + i) % n
-        total = contract(normed[:, at(place, 1 + r, block)], grads[...], 0, 0)
+        total = contract(normed[:, at(place, 1 + n + k + r, block)], grads[...], 0, 0)
         outs[r][...] = total.astype(outs[r].dtype)
 
 
@@ -780,7 +792,13 @@
     _, rows, width = hidden_in.shape
     share = rows // k
     block = width // n
-    place = scalars(ctx, *[(shard - r) % n for r in range(n)], *[ten ^ o for o in t_offsets])
+    place = scalars(
+        ctx,
+        *[(shard - r) % n for r in range(n)],
+        *[ten ^ o for o in t_offsets],
+        *[shard ^ o for o in range(n)],
+    )
+    ring_places = scalars(*[(shard - (shard ^ o)) % n for o in range(n)])
     hidden, cot = hidden_in[0], cotangent[0]
 
     kv_part = key_weight.shape[1] // HEAD // m
@@ -818,9 +836,7 @@
     seg_row = segment_ids
     seg_col = segment_ids.reshape(-1, 1)
 
-    normed_one = call(
-        lambda *refs: norm_kernel(n, k, *refs), shaped((rows, width), BF), (place, hidden, gains)
-    )
+    normed_one = call(lambda *refs: norm_kernel(n, k, *refs), shaped((rows, width), BF), (place, hidden, gains))
     out_mine = after(out_mine, middle_piece)
     out_firsts = []
     for r in range(1, n):
@@ -930,8 +946,6 @@
         for i in range(n):
             r = (1 + i) % n
             if j:
-                if i >= n // 2:
-                    parts[r] = after(parts[r], unit_terms[1 + i - n // 2][0])
                 parts[r] = send_part(parts[r], j)
             unit_terms[r].append(parts[r])
     unit_totals = []
@@ -964,22 +978,20 @@
     for o, sent in zip(c_offsets[1:], kv_sends):
         kv_received.append(swap(sent, CX, o))
     out_grads = call(
-        lambda *refs: out_grad_kernel(n, m, *refs),
-        [shaped((m * q_cols, block), BF if r == 1 % n else F32) for r in range(n)],
+        lambda *refs: out_grad_kernel(n, m, k, *refs),
+        [shaped((m * q_cols, block), BF if r % 2 else F32) for r in range(n)],
         (place, attended, after(all_grads, kv_grad)),
     )
     feed_bits = xor_bits(k)
+    assert len(feed_bits) == 2
     for i, bit in enumerate(feed_bits):
         if i + 1 == len(feed_bits):
             feed_high = after(feed_high, kv_grad)
         feed_received = swap(feed_high, TN, bit)
         if i + 1 < len(feed_bits):
-            feed_low, feed_high = feed_add(place, after(feed_low, kv_grad), feed_received)
+            feed_low, feed_high = feed_add(ring_places, feed_low, feed_received)
     feed_sum = feed_low.astype(F32) + feed_received.astype(F32)
-    total = feed_sum[1 % n]
-    for r in range(2, n + 1):
-        moved_on = shift(total.astype(BF), 1)
-        total = moved_on.astype(F32) + feed_sum[r % n]
+    total = shard_sum([feed_sum[o] for o in range(n)])
     layer_out = (residual + total).astype(BF)[None]
 
     qkv_grads = call(
@@ -990,19 +1002,15 @@
     terms = [[] for _ in range(n)]
     for j in reversed(range(m)):
         parts = list(call(
-            lambda *refs: qkv_grad_kernel(n, *refs),
+            lambda *refs: qkv_grad_kernel(n, k, *refs),
             [shaped((block, part_cols), BF if j else F32)] * n,
             (place, normed_one, qkv_grads[j]),
         ))
-        for i in range(n):
-            r = (1 + i) % n
+        for r in list(range(1, n, 2)) + list(range(0, n, 2)):
             if j:
                 parts[r] = send_part(parts[r], j)
             terms[r].append(parts[r])
-    total = after(out_grads[1 % n], terms[0][-1])
-    for r in range(2, n + 1):
-        total = shift(total.astype(BF), 1)
-        total = total.astype(F32) + out_grads[r % n]
+    total = shard_sum(out_grads)
     parts = [total[j * q_cols : (j + 1) * q_cols] for j in range(m)]
     sums = list(parts)
     for o in c_offsets[1:]:
@@ -1012,20 +1020,14 @@
     grad_output_out = join_rows([s[None] for s in sums])
     unit_parts = []
     for r in range(n):
-        unit_parts.append(gather_direct(after(unit_totals[r], terms[0][-1] if r else kv_grad)))
+        unit_parts.append(gather_direct(after(unit_totals[r], terms[0][-1] if r > 1 else grad_b)))
     low, high = call(
         lambda *refs: qkv_back_kernel(n, m, *refs),
         [shaped((rows // 2, width), F32), shaped((rows // 2, width), BF)],
         (place, *qkv_grads, *flat_qkv),
     )
     kept, received = scatter_open(low, high)
-    total = None
-    for i in range(n):
-        r = (1 + i) % n
-        term = sum(t.astype(F32) for t in terms[r])
-        if r:
-            term = shift(term.astype(BF), -r).astype(F32)
-        total = term if total is None else total + term
+    total = shard_sum([sum(t.astype(F32) for t in term) for term in terms])
     qkv_parts_out = gather_direct(total.astype(BF))
     grad_query_out, grad_key_out, grad_value_out = call(
         lambda *refs: qkv_join_kernel(m, c_offsets, q_cols, kv_cols, *refs),

time: 741 us -> 722 us (0.974)
  waiting for transfers between devices: 368 us -> 347 us
  starting transfers between devices: 113 us -> 121 us
    ppermute x33 -> x24, waiting for transfers between devices: 240 us -> 176 us  [shift(): lax.ppermute(value, SH, [(i, (i + steps) % size) for i in range(size)])]
    ppermute x55 -> x61, waiting for transfers between devices: 128 us -> 171 us  [swap(): return lax.ppermute(value, axis, [(i, i ^ offset) for i in range(size)])]
    ppermute x55 -> x61, starting transfers between devices: 44.3 us -> 59.6 us  [swap(): return lax.ppermute(value, axis, [(i, i ^ offset) for i in range(size)])]
    another operation x0 -> x7, other arithmetic: none -> 8.22 us  [the longest x5 4.36 us: shard_sum(): got = swap(jnp.stack(sent) if len(sent) > 1 else sent[0][None], SH, bit)]
    ppermute x33 -> x24, starting transfers between devices: 69 us -> 61.3 us  [shift(): lax.ppermute(value, SH, [(i, (i + steps) % size) for i in range(size)])]
  transfers between devices with their start and end apart: 88 -> 85, of which waited for: 34 -> 33; matrix products, arithmetic and copies ran while one was open for 6% -> 5% of each run, Pallas kernels for 24% -> 24%
where the time goes in v2:
time: 722 us; the launch traced here: 718 us
  waiting for transfers between devices  347 us (48%)
  Pallas kernels  202 us (28%)
  starting transfers between devices  121 us (17%)
  other arithmetic  26 us (4%)
  local copies, waits for them, and re-layouts  20.8 us (3%)
    ppermute x24, waiting for transfers between devices, shift(): lax.ppermute(value, SH, [(i, (i + steps) % size) for i in range(size)])  176 us
    ppermute x61, waiting for transfers between devices, swap(): return lax.ppermute(value, axis, [(i, i ^ offset) for i in range(size)])  171 us
    pallas_call x15, Pallas kernels, call(): pl.pallas_call(kernel, out_shape=outs, in_specs=[pl.BlockSpec(memory_spac...  80.6 us
    ppermute x24, starting transfers between devices, shift(): lax.ppermute(value, SH, [(i, (i + steps) % size) for i in range(size)])  61.3 us
    ppermute x61, starting transfers between devices, swap(): return lax.ppermute(value, axis, [(i, i ^ offset) for i in range(size)])  59.6 us
    pallas_call x4, Pallas kernels, mlp_chunk(): pl.pallas_call(lambda *refs: mlp_kernel(first, r, n, k, m, refs), out_sha...  48.7 us
    pallas_call x3, Pallas kernels, unit_grads(): pl.pallas_call(lambda *refs: unit_grad_kernel(count, *refs), out_shape=[o...  32.4 us
  transfers between devices with their start and end apart: 85, of which 33 were waited for; matrix products, arithmetic and copies ran while one was open for 5% of the time, Pallas kernels for 24%

profile of v2, /device:TPU:0, one launch (start us, length us, event | category | flops | bytes accessed | tf_op | source)
XLA Modules:
  0.0 718.2 jit_solution(18125333874434037071)
XLA Ops:
  41.7 12.3 %collective-permute-done.10.refs_3_.refs_6_ = bf16[256,512]{1,0:T(8,128)(2,1)S(1)} collective-permute-done((bf16[256,512]{1,0:T(8,128)(2,1)S(1)}, bf16[256,512]{1,0:T(8,128)(2,1)S(1)}, u32[]{:S(2)}, u32[]{:S(2)}) %collective-permute-start.10) | collective-permute-done | bytes 262176 | tf_op jit(solution)/shard_map/ppermute | solution.py:50
  76.4 17.8 %collective-permute-done.9.refs_5_.refs_8_ = bf16[512,256]{1,0:T(8,128)(2,1)S(1)} collective-permute-done((bf16[512,256]{1,0:T(8,128)(2,1)}, bf16[512,256]{1,0:T(8,128)(2,1)S(1)}, u32[]{:S(2)}, u32[]{:S(2)}) %collective-permute-start.9) | collective-permute-done | bytes 262176 | tf_op jit(solution)/shard_map/ppermute | solution.py:45
  94.9 8.9 %shard_map.223 = (bf16[512,512]{1,0:T(8,128)(2,1)}, f32[512,128]{1,0:T(8,128)}) custom-call(s32[13]{0:T(128)} %stack.112.refs_0_.place, bf16[512,512]{1,0:T(8,128)(2,1)} %get-tuple-element.140.refs_1_, s32[1,1024]{1,0:T(1,128)} %refs_2_.9, s32[1024,1]{1,0:T(8,128)} %copy.52.refs_3_, bf16[512,256]{1,0:T(8,128)(2,1)} %get-tuple-element.143.refs_4_.refs_7_, ...), custom_call_target="tpu_custom_call" | custom-call | tf_op jit(solution)/shard_map/pallas_call | solution.py:479
  122.9 11.4 %collective-permute-done.15.received = bf16[128,2048]{1,0:T(8,128)(2,1)S(1)} collective-permute-done((bf16[128,2048]{1,0:T(8,128)(2,1)S(1)}, bf16[128,2048]{1,0:T(8,128)(2,1)S(1)}, u32[]{:S(2)}, u32[]{:S(2)}) %collective-permute-start.15) | collective-permute-done | bytes 524320 | tf_op jit(solution)/shard_map/ppermute | solution.py:45
  138.5 16.6 %collective-permute-done.16.refs_13_.refs_9_.refs_7_ = bf16[768,512]{1,0:T(8,128)(2,1)S(1)} collective-permute-done((bf16[768,512]{1,0:T(8,128)(2,1)}, bf16[768,512]{1,0:T(8,128)(2,1)S(1)}, u32[]{:S(2)}, u32[]{:S(2)}) %collective-permute-start.16) | collective-permute-done | bytes 786464 | tf_op jit(solution)/shard_map/ppermute | solution.py:50
  159.6 23.6 %collective-permute-done.17.refs_1_ = bf16[256,2048]{1,0:T(8,128)(2,1)S(1)} collective-permute-done((bf16[256,2048]{1,0:T(8,128)(2,1)}, bf16[256,2048]{1,0:T(8,128)(2,1)S(1)}, u32[]{:S(2)}, u32[]{:S(2)}) %collective-permute-start.17) | collective-permute-done | bytes 1048608 | tf_op jit(solution)/shard_map/ppermute | solution.py:50
  183.2 16.8 %collective-permute-done.23.refs_11_.refs_7_.refs_5_ = bf16[768,512]{1,0:T(8,128)(2,1)S(1)} collective-permute-done((bf16[768,512]{1,0:T(8,128)(2,1)S(1)}, bf16[768,512]{1,0:T(8,128)(2,1)S(1)}, u32[]{:S(2)}, u32[]{:S(2)}) %collective-permute-start.23) | collective-permute-done | bytes 786464 | tf_op jit(solution)/shard_map/ppermute | solution.py:50
  203.0 13.8 %collective-permute-done.26.refs_15_.refs_11_.refs_9_ = bf16[768,512]{1,0:T(8,128)(2,1)S(1)} collective-permute-done((bf16[768,512]{1,0:T(8,128)(2,1)S(1)}, bf16[768,512]{1,0:T(8,128)(2,1)S(1)}, u32[]{:S(2)}, u32[]{:S(2)}) %collective-permute-start.26) | collective-permute-done | bytes 786464 | tf_op jit(solution)/shard_map/ppermute | solution.py:50
  220.4 17.7 %collective-permute-done.18.refs_1_ = bf16[256,2048]{1,0:T(8,128)(2,1)S(1)} collective-permute-done((bf16[256,2048]{1,0:T(8,128)(2,1)S(1)}, bf16[256,2048]{1,0:T(8,128)(2,1)S(1)}, u32[]{:S(2)}, u32[]{:S(2)}) %collective-permute-start.18) | collective-permute-done | bytes 1048608 | tf_op jit(solution)/shard_map/ppermute | solution.py:50
  239.7 13.3 %collective-permute-done.25.refs_14_.refs_10_.refs_8_ = bf16[768,512]{1,0:T(8,128)(2,1)S(1)} collective-permute-done((bf16[768,512]{1,0:T(8,128)(2,1)S(1)}, bf16[768,512]{1,0:T(8,128)(2,1)S(1)}, u32[]{:S(2)}, u32[]{:S(2)}) %collective-permute-start.25) | collective-permute-done | bytes 786464 | tf_op jit(solution)/shard_map/ppermute | solution.py:45
  253.5 10.4 %collective-permute-done.19.refs_1_ = bf16[256,2048]{1,0:T(8,128)(2,1)S(1)} collective-permute-done((bf16[256,2048]{1,0:T(8,128)(2,1)S(1)}, bf16[256,2048]{1,0:T(8,128)(2,1)S(1)}, u32[]{:S(2)}, u32[]{:S(2)}) %collective-permute-start.19) | collective-permute-done | bytes 1048608 | tf_op jit(solution)/shard_map/ppermute | solution.py:50
  267.6 12.0 %mc.4 = (bf16[2048,2048]{1,0:T(8,128)(2,1)}, bf16[2048,2048]{1,0:T(8,128)(2,1)}, bf16[2048,256]{1,0:T(8,128)(2,1)}, bf16[2048,256]{1,0:T(8,128)(2,1)}, bf16[2048...) custom-call(s32[13]{0:T(128)} %stack.112.refs_0_.place, ...), custom_call_target="tpu_custom_call" | custom-call | tf_op jit(solution)/shard_map/mc/pallas_call | solution.py:214
  280.3 9.1 %collective-permute-done.20.refs_2_ = bf16[256,2048]{1,0:T(8,128)(2,1)} collective-permute-done((bf16[256,2048]{1,0:T(8,128)(2,1)S(1)}, bf16[256,2048]{1,0:T(8,128)(2,1)}, u32[]{:S(2)}, u32[]{:S(2)}) %collective-permute-start.20) | collective-permute-done | bytes 1048608 | tf_op jit(solution)/shard_map/ppermute | solution.py:45
  289.4 12.1 %mc.5 = (bf16[2048,2048]{1,0:T(8,128)(2,1)}, bf16[2048,2048]{1,0:T(8,128)(2,1)}, bf16[2048,256]{1,0:T(8,128)(2,1)}, bf16[2048,256]{1,0:T(8,128)(2,1)}, bf16[2048...) custom-call(s32[13]{0:T(128)} %stack.112.refs_0_.place, ...), custom_call_target="tpu_custom_call", output_to_operand_aliasing={{0}: (13, {}), {1}: (14, {}), {2}: (15, {}), {3}: (16, {}),... | custom-call | tf_op jit(solution)/shard_map/mc/pallas_call | solution.py:214
  302.1 12.4 %mc.6 = (bf16[2048,2048]{1,0:T(8,128)(2,1)}, bf16[2048,2048]{1,0:T(8,128)(2,1)}, bf16[2048,256]{1,0:T(8,128)(2,1)}, bf16[2048,256]{1,0:T(8,128)(2,1)}, bf16[2048...) custom-call(s32[13]{0:T(128)} %stack.112.refs_0_.place, ...), custom_call_target="tpu_custom_call", output_to_operand_aliasing={{0}: (13, {}), {1}: (14, {}), {2}: (15, {}), {3}: (16, {}),... | custom-call | tf_op jit(solution)/shard_map/mc/pallas_call | solution.py:214
  316.6 12.2 %mc.7 = (bf16[2048,2048]{1,0:T(8,128)(2,1)}, bf16[2048,2048]{1,0:T(8,128)(2,1)}, bf16[2048,256]{1,0:T(8,128)(2,1)}, bf16[2048,256]{1,0:T(8,128)(2,1)}, bf16[2048...) custom-call(s32[13]{0:T(128)} %stack.112.refs_0_.place, ...), custom_call_target="tpu_custom_call", output_to_operand_aliasing={{0}: (13, {}), {1}: (14, {}), {2}: (15, {}), {3}: (16, {}),... | custom-call | tf_op jit(solution)/shard_map/mc/pallas_call | solution.py:214
  335.1 9.2 %collective-permute-done.40 = bf16[128,2048]{1,0:T(8,128)(2,1)S(1)} collective-permute-done((bf16[128,2048]{1,0:T(8,128)(2,1)S(1)}, bf16[128,2048]{1,0:T(8,128)(2,1)S(1)}, u32[]{:S(2)}, u32[]{:S(2)}) %collective-permute-start.40) | collective-permute-done | bytes 524320 | tf_op jit(solution)/shard_map/ppermute | solution.py:45
  344.4 20.1 %collective-permute-start.41 = (bf16[128,2048]{1,0:T(8,128)(2,1)S(1)}, bf16[128,2048]{1,0:T(8,128)(2,1)S(1)}, u32[]{:S(2)}, u32[]{:S(2)}) collective-permute-start(bf16[128,2048]{1,0:T(8,128)(2,1)S(1)} %fusion.7), channel_id=1, source_target_pairs={{0,24},{8,0},{16,8},{24,16},{1,25},{9,1},{17,9},{25,17},{2,26},{10... | collective-permute-start | bytes 1572872 | tf_op jit(solution)/shard_map/ppermute | solution.py:50
  364.6 9.2 %collective-permute-start.44 = (bf16[128,2048]{1,0:T(8,128)(2,1)S(1)}, bf16[128,2048]{1,0:T(8,128)(2,1)S(1)}, u32[]{:S(2)}, u32[]{:S(2)}) collective-permute-start(bf16[128,2048]{1,0:T(8,128)(2,1)S(1)} %fusion.6), channel_id=1, source_target_pairs={{0,16},{8,24},{16,0},{24,8},{1,17},{9,25},{17,1},{25,9},{2,18},{10... | collective-permute-start | bytes 1572872 | tf_op jit(solution)/shard_map/ppermute | solution.py:50
  378.0 29.2 %collective-permute-done.44.refs_1_ = bf16[128,2048]{1,0:T(8,128)(2,1)S(1)} collective-permute-done((bf16[128,2048]{1,0:T(8,128)(2,1)S(1)}, bf16[128,2048]{1,0:T(8,128)(2,1)S(1)}, u32[]{:S(2)}, u32[]{:S(2)}) %collective-permute-start.44) | collective-permute-done | bytes 524320 | tf_op jit(solution)/shard_map/ppermute | solution.py:50
  412.5 9.5 %fo.1 = (bf16[4,256,2048]{2,1,0:T(8,128)(2,1)}, bf16[4,256,2048]{2,1,0:T(8,128)(2,1)}) custom-call(s32[13]{0:T(128)} %stack.112.refs_0_.place, bf16[4,512,256]{2,1,0:T(8,128)(2,1)} %bitcast.95, bf16[4,512,256]{2,1,0:T(8,128)(2,1)} %bitcast.94, bf16[768,512]{1,0:T(8,128)(2,1)} %get-tuple-element.157.refs_9_.refs_5_.refs_3_, ...), custom_call_target="tpu_custom_call" | custom-call | tf_op jit(solution)/shard_map/fo/pallas_call | solution.py:256
  422.1 8.9 %shard_map.238 = (bf16[768,512]{1,0:T(8,128)(2,1)}, bf16[768,512]{1,0:T(8,128)(2,1)}) custom-call(s32[13]{0:T(128)} %stack.112.refs_0_.place, bf16[2048,2048]{1,0:T(8,128)(2,1)} %get-tuple-element.235.refs_1_, bf16[2048,2048]{1,0:T(8,128)(2,1)} %get-tuple-element.236.refs_2_, bf16[2048,256]{1,0:T(8,128)(2,1)} %get-tuple-element.199.refs_3_, ...), custom_call_target="tpu_custom_call" | custom-call | tf_op jit(solution)/shard_map/pallas_call | solution.py:352
  433.0 8.9 %shard_map.236 = (bf16[768,512]{1,0:T(8,128)(2,1)}, bf16[768,512]{1,0:T(8,128)(2,1)}) custom-call(s32[13]{0:T(128)} %stack.112.refs_0_.place, bf16[2048,2048]{1,0:T(8,128)(2,1)} %get-tuple-element.235.refs_1_, bf16[2048,2048]{1,0:T(8,128)(2,1)} %get-tuple-element.236.refs_2_, bf16[2048,256]{1,0:T(8,128)(2,1)} %get-tuple-element.199.refs_3_, ...), custom_call_target="tpu_custom_call" | custom-call | tf_op jit(solution)/shard_map/pallas_call | solution.py:352
  443.9 14.7 %shard_map.237 = (f32[768,512]{1,0:T(8,128)}, f32[768,512]{1,0:T(8,128)}, f32[768,512]{1,0:T(8,128)}, f32[768,512]{1,0:T(8,128)}) custom-call(s32[13]{0:T(128)} %stack.112.refs_0_.place, bf16[2048,2048]{1,0:T(8,128)(2,1)} %get-tuple-element.235.refs_1_, bf16[2048,2048]{1,0:T(8,128)(2,1)} %get-tuple-element.236.refs_2_, ...), custom_call_target="tpu_custom_call" | custom-call | tf_op jit(solution)/shard_map/pallas_call | solution.py:352
  459.2 9.2 %collective-permute-done.77 = bf16[768,512]{1,0:T(8,128)(2,1)S(1)} collective-permute-done((bf16[768,512]{1,0:T(8,128)(2,1)}, bf16[768,512]{1,0:T(8,128)(2,1)S(1)}, u32[]{:S(2)}, u32[]{:S(2)}) %collective-permute-start.77) | collective-permute-done | bytes 786464 | tf_op jit(solution)/shard_map/ppermute | solution.py:45
  470.1 15.2 %collective-permute-done.74 = bf16[768,512]{1,0:T(8,128)(2,1)S(1)} collective-permute-done((bf16[768,512]{1,0:T(8,128)(2,1)}, bf16[768,512]{1,0:T(8,128)(2,1)S(1)}, u32[]{:S(2)}, u32[]{:S(2)}) %collective-permute-start.74) | collective-permute-done | bytes 786464 | tf_op jit(solution)/shard_map/ppermute | solution.py:45
  497.9 17.4 %shard_map.228 = (f32[512,512]{1,0:T(8,128)}, f32[512,256]{1,0:T(8,128)}, bf16[512,256]{1,0:T(8,128)(2,1)}) custom-call(s32[13]{0:T(128)} %stack.112.refs_0_.place, bf16[512,512]{1,0:T(8,128)(2,1)} %get-tuple-element.140.refs_1_, s32[1,1024]{1,0:T(1,128)} %refs_2_.9, s32[1024,1]{1,0:T(8,128)} %copy.52.refs_3_, ...), custom_call_target="tpu_custom_call" | custom-call | tf_op jit(solution)/shard_map/pallas_call | solution.py:479
  537.9 19.3 %collective-permute-done.78.refs_1_ = bf16[768,512]{1,0:T(8,128)(2,1)} collective-permute-done((bf16[768,512]{1,0:T(8,128)(2,1)S(1)}, bf16[768,512]{1,0:T(8,128)(2,1)}, u32[]{:S(2)}, u32[]{:S(2)}) %collective-permute-start.78) | collective-permute-done | bytes 786464 | tf_op jit(solution)/shard_map/ppermute | solution.py:50
  599.5 12.2 %collective-permute-done.76.refs_2_ = bf16[768,512]{1,0:T(8,128)(2,1)} collective-permute-done((bf16[768,512]{1,0:T(8,128)(2,1)S(1)}, bf16[768,512]{1,0:T(8,128)(2,1)}, u32[]{:S(2)}, u32[]{:S(2)}) %collective-permute-start.76) | collective-permute-done | bytes 786464 | tf_op jit(solution)/shard_map/ppermute | solution.py:45
  625.5 15.5 %collective-permute-done.67 = bf16[2,512,384]{2,1,0:T(8,128)(2,1)S(1)} collective-permute-done((bf16[2,512,384]{2,1,0:T(8,128)(2,1)}, bf16[2,512,384]{2,1,0:T(8,128)(2,1)S(1)}, u32[]{:S(2)}, u32[]{:S(2)}) %collective-permute-start.67) | collective-permute-done | bytes 786464 | tf_op jit(solution)/shard_map/ppermute | solution.py:45
  674.0 8.7 %collective-permute-done.60 = f32[2,2048]{1,0:T(2,128)S(1)} collective-permute-done((f32[2,2048]{1,0:T(2,128)S(1)}, f32[2,2048]{1,0:T(2,128)S(1)}, u32[]{:S(2)}, u32[]{:S(2)}) %collective-permute-start.60) | collective-permute-done | bytes 16416 | tf_op jit(solution)/shard_map/ppermute | solution.py:45
  701.7 15.2 %collective-permute-done.54 = bf16[1,128,2048]{2,1,0:T(8,128)(2,1)S(1)} collective-permute-done((bf16[1,128,2048]{2,1,0:T(8,128)(2,1)S(1)}, bf16[1,128,2048]{2,1,0:T(8,128)(2,1)S(1)}, u32[]{:S(2)}, u32[]{:S(2)}) %collective-permute-start.54) | collective-permute-done | bytes 524320 | tf_op jit(solution)/shard_map/ppermute | solution.py:45
  (369 shorter events, 273.5 us)
Async XLA Ops:
  114.7 40.4 %collective-permute-start.16 = (bf16[768,512]{1,0:T(8,128)(2,1)}, bf16[768,512]{1,0:T(8,128)(2,1)S(1)}, u32[]{:S(2)}, u32[]{:S(2)}) collective-permute-start(bf16[768,512]{1,0:T(8,128)(2,1)} %get-tuple-element.155), channel_id=1, source_target_pairs={{0,16},{8,24},{16,0},{24,8},{1,17},{9,25},{17,1},{25,9},{2,18},{10... | collective-permute-start | bytes 2359304 | tf_op jit(solution)/shard_map/ppermute | solution.py:50
  155.7 44.3 %collective-permute-start.23 = (bf16[768,512]{1,0:T(8,128)(2,1)S(1)}, bf16[768,512]{1,0:T(8,128)(2,1)S(1)}, u32[]{:S(2)}, u32[]{:S(2)}) collective-permute-start(bf16[768,512]{1,0:T(8,128)(2,1)S(1)} %copy-done.64), channel_id=1, source_target_pairs={{0,8},{8,16},{16,24},{24,0},{1,9},{9,17},{17,25},{25,1},{2,10},{10... | collective-permute-start | bytes 2359304 | tf_op jit(solution)/shard_map/ppermute | solution.py:50
  155.8 61.0 %collective-permute-start.26 = (bf16[768,512]{1,0:T(8,128)(2,1)S(1)}, bf16[768,512]{1,0:T(8,128)(2,1)S(1)}, u32[]{:S(2)}, u32[]{:S(2)}) collective-permute-start(bf16[768,512]{1,0:T(8,128)(2,1)S(1)} %copy-done.63), channel_id=1, source_target_pairs={{0,24},{8,0},{16,8},{24,16},{1,25},{9,1},{17,9},{25,17},{2,26},{10... | collective-permute-start | bytes 2359304 | tf_op jit(solution)/shard_map/ppermute | solution.py:50
  183.2 54.9 %collective-permute-start.18 = (bf16[256,2048]{1,0:T(8,128)(2,1)S(1)}, bf16[256,2048]{1,0:T(8,128)(2,1)S(1)}, u32[]{:S(2)}, u32[]{:S(2)}) collective-permute-start(bf16[256,2048]{1,0:T(8,128)(2,1)S(1)} %collective-permute-done.17.refs_1_), channel_id=1, source_target_pairs={{0,8},{8,16},{16,24},{24,0},{1,9},{9,17},{17,25},{25,1},{2,10},{10... | collective-permute-start | bytes 3145736 | tf_op jit(solution)/shard_map/ppermute | solution.py:50
  218.3 34.7 %collective-permute-start.25 = (bf16[768,512]{1,0:T(8,128)(2,1)S(1)}, bf16[768,512]{1,0:T(8,128)(2,1)S(1)}, u32[]{:S(2)}, u32[]{:S(2)}) collective-permute-start(bf16[768,512]{1,0:T(8,128)(2,1)S(1)} %collective-permute-done.16.refs_13_.refs_9_.refs_7_), channel_id=1, source_target_pairs={{0,4},{4,0},{1,5},{5,1},{2,6},{6,2},{3,7},{7,3},{8,12},{12,8},{9,1... | collective-permute-start | bytes 2359304 | tf_op jit(solution)/shard_map/ppermute | solution.py:45
  218.8 34.2 %collective-permute-start.31 = (bf16[256,2048]{1,0:T(8,128)(2,1)S(1)}, bf16[256,2048]{1,0:T(8,128)(2,1)}, u32[]{:S(2)}, u32[]{:S(2)}) collective-permute-start(bf16[256,2048]{1,0:T(8,128)(2,1)S(1)} %collective-permute-done.17.refs_1_), channel_id=1, source_target_pairs={{0,2},{1,3},{2,0},{3,1},{4,6},{5,7},{6,4},{7,5},{8,10},{9,11},{10,... | collective-permute-start | bytes 3145736 | tf_op jit(solution)/shard_map/ppermute | solution.py:45
  239.7 39.9 %collective-permute-start.32 = (bf16[256,2048]{1,0:T(8,128)(2,1)S(1)}, bf16[256,2048]{1,0:T(8,128)(2,1)}, u32[]{:S(2)}, u32[]{:S(2)}) collective-permute-start(bf16[256,2048]{1,0:T(8,128)(2,1)S(1)} %collective-permute-done.17.refs_1_), channel_id=1, source_target_pairs={{0,1},{1,0},{2,3},{3,2},{4,5},{5,4},{6,7},{7,6},{8,9},{9,8},{10,11... | collective-permute-start | bytes 3145736 | tf_op jit(solution)/shard_map/ppermute | solution.py:45
  265.4 36.1 %collective-permute-start.29 = (bf16[256,2048]{1,0:T(8,128)(2,1)S(1)}, bf16[256,2048]{1,0:T(8,128)(2,1)}, u32[]{:S(2)}, u32[]{:S(2)}) collective-permute-start(bf16[256,2048]{1,0:T(8,128)(2,1)S(1)} %collective-permute-done.18.refs_1_), channel_id=1, source_target_pairs={{0,1},{1,0},{2,3},{3,2},{4,5},{5,4},{6,7},{7,6},{8,9},{9,8},{10,11... | collective-permute-start | bytes 3145736 | tf_op jit(solution)/shard_map/ppermute | solution.py:45
  267.5 34.6 %collective-permute-start.30 = (bf16[256,2048]{1,0:T(8,128)(2,1)}, bf16[256,2048]{1,0:T(8,128)(2,1)}, u32[]{:S(2)}, u32[]{:S(2)}) collective-permute-start(bf16[256,2048]{1,0:T(8,128)(2,1)} %collective-permute-done.28.refs_2_), channel_id=1, source_target_pairs={{0,1},{1,0},{2,3},{3,2},{4,5},{5,4},{6,7},{7,6},{8,9},{9,8},{10,11... | collective-permute-start | bytes 3145736 | tf_op jit(solution)/shard_map/ppermute | solution.py:45
  279.6 35.0 %collective-permute-start.37 = (bf16[256,2048]{1,0:T(8,128)(2,1)}, bf16[256,2048]{1,0:T(8,128)(2,1)S(1)}, u32[]{:S(2)}, u32[]{:S(2)}) collective-permute-start(bf16[256,2048]{1,0:T(8,128)(2,1)} %get-tuple-element.189), channel_id=1, source_target_pairs={{0,1},{1,0},{2,3},{3,2},{4,5},{5,4},{6,7},{7,6},{8,9},{9,8},{10,11... | collective-permute-start | bytes 3145736 | tf_op jit(solution)/shard_map/ppermute | solution.py:45
  280.2 36.4 %collective-permute-start.21 = (bf16[256,2048]{1,0:T(8,128)(2,1)S(1)}, bf16[256,2048]{1,0:T(8,128)(2,1)}, u32[]{:S(2)}, u32[]{:S(2)}) collective-permute-start(bf16[256,2048]{1,0:T(8,128)(2,1)S(1)} %collective-permute-done.19.refs_1_), channel_id=1, source_target_pairs={{0,1},{1,0},{2,3},{3,2},{4,5},{5,4},{6,7},{7,6},{8,9},{9,8},{10,11... | collective-permute-start | bytes 3145736 | tf_op jit(solution)/shard_map/ppermute | solution.py:45
  315.1 62.9 %collective-permute-start.38 = (bf16[128,2048]{1,0:T(8,128)(2,1)S(1)}, bf16[128,2048]{1,0:T(8,128)(2,1)S(1)}, u32[]{:S(2)}, u32[]{:S(2)}) collective-permute-start(bf16[128,2048]{1,0:T(8,128)(2,1)S(1)} %slice.191), channel_id=1, source_target_pairs={{0,2},{1,3},{2,0},{3,1},{4,6},{5,7},{6,4},{7,5},{8,10},{9,11},{10,... | collective-permute-start | bytes 1572872 | tf_op jit(solution)/shard_map/ppermute | solution.py:45
  332.5 32.0 %collective-permute-start.43 = (bf16[128,2048]{1,0:T(8,128)(2,1)S(1)}, bf16[128,2048]{1,0:T(8,128)(2,1)S(1)}, u32[]{:S(2)}, u32[]{:S(2)}) collective-permute-start(bf16[128,2048]{1,0:T(8,128)(2,1)S(1)} %slice.189), channel_id=1, source_target_pairs={{0,2},{1,3},{2,0},{3,1},{4,6},{5,7},{6,4},{7,5},{8,10},{9,11},{10,... | collective-permute-start | bytes 1572872 | tf_op jit(solution)/shard_map/ppermute | solution.py:45
  333.8 40.0 %collective-permute-start.46 = (bf16[128,2048]{1,0:T(8,128)(2,1)S(1)}, bf16[128,2048]{1,0:T(8,128)(2,1)S(1)}, u32[]{:S(2)}, u32[]{:S(2)}) collective-permute-start(bf16[128,2048]{1,0:T(8,128)(2,1)S(1)} %slice.188), channel_id=1, source_target_pairs={{0,2},{1,3},{2,0},{3,1},{4,6},{5,7},{6,4},{7,5},{8,10},{9,11},{10,... | collective-permute-start | bytes 1572872 | tf_op jit(solution)/shard_map/ppermute | solution.py:45
  344.4 33.6 %collective-permute-start.41 = (bf16[128,2048]{1,0:T(8,128)(2,1)S(1)}, bf16[128,2048]{1,0:T(8,128)(2,1)S(1)}, u32[]{:S(2)}, u32[]{:S(2)}) collective-permute-start(bf16[128,2048]{1,0:T(8,128)(2,1)S(1)} %fusion.7), channel_id=1, source_target_pairs={{0,24},{8,0},{16,8},{24,16},{1,25},{9,1},{17,9},{25,17},{2,26},{10... | collective-permute-start | bytes 1572872 | tf_op jit(solution)/shard_map/ppermute | solution.py:50
  364.6 42.6 %collective-permute-start.44 = (bf16[128,2048]{1,0:T(8,128)(2,1)S(1)}, bf16[128,2048]{1,0:T(8,128)(2,1)S(1)}, u32[]{:S(2)}, u32[]{:S(2)}) collective-permute-start(bf16[128,2048]{1,0:T(8,128)(2,1)S(1)} %fusion.6), channel_id=1, source_target_pairs={{0,16},{8,24},{16,0},{24,8},{1,17},{9,25},{17,1},{25,9},{2,18},{10... | collective-permute-start | bytes 1572872 | tf_op jit(solution)/shard_map/ppermute | solution.py:50
  373.9 33.3 %collective-permute-start.47 = (bf16[128,2048]{1,0:T(8,128)(2,1)S(1)}, bf16[128,2048]{1,0:T(8,128)(2,1)S(1)}, u32[]{:S(2)}, u32[]{:S(2)}) collective-permute-start(bf16[128,2048]{1,0:T(8,128)(2,1)S(1)} %fusion.5), channel_id=1, source_target_pairs={{0,8},{8,16},{16,24},{24,0},{1,9},{9,17},{17,25},{25,1},{2,10},{10... | collective-permute-start | bytes 1572872 | tf_op jit(solution)/shard_map/ppermute | solution.py:50
  422.1 155.0 %collective-permute-start.48 = (bf16[4,256,2048]{2,1,0:T(8,128)(2,1)}, bf16[4,256,2048]{2,1,0:T(8,128)(2,1)}, u32[]{:S(2)}, u32[]{:S(2)}) collective-permute-start(bf16[4,256,2048]{2,1,0:T(8,128)(2,1)} %get-tuple-element.201), channel_id=1, source_target_pairs={{0,1},{1,0},{2,3},{3,2},{4,5},{5,4},{6,7},{7,6},{8,9},{9,8},{10,11... | collective-permute-start | bytes 12582920 | tf_op jit(solution)/shard_map/ppermute | solution.py:45
  432.5 36.0 %collective-permute-start.77 = (bf16[768,512]{1,0:T(8,128)(2,1)}, bf16[768,512]{1,0:T(8,128)(2,1)S(1)}, u32[]{:S(2)}, u32[]{:S(2)}) collective-permute-start(bf16[768,512]{1,0:T(8,128)(2,1)} %get-tuple-element.242), channel_id=1, source_target_pairs={{0,4},{4,0},{1,5},{5,1},{2,6},{6,2},{3,7},{7,3},{8,12},{12,8},{9,1... | collective-permute-start | bytes 2359304 | tf_op jit(solution)/shard_map/ppermute | solution.py:45
  441.8 43.4 %collective-permute-start.74 = (bf16[768,512]{1,0:T(8,128)(2,1)}, bf16[768,512]{1,0:T(8,128)(2,1)S(1)}, u32[]{:S(2)}, u32[]{:S(2)}) collective-permute-start(bf16[768,512]{1,0:T(8,128)(2,1)} %get-tuple-element.238), channel_id=1, source_target_pairs={{0,4},{4,0},{1,5},{5,1},{2,6},{6,2},{3,7},{7,3},{8,12},{12,8},{9,1... | collective-permute-start | bytes 2359304 | tf_op jit(solution)/shard_map/ppermute | solution.py:45
  443.3 45.5 %collective-permute-start.49 = (bf16[128,2048]{1,0:T(8,128)(2,1)S(1)}, bf16[128,2048]{1,0:T(8,128)(2,1)S(1)}, u32[]{:S(2)}, u32[]{:S(2)}) collective-permute-start(bf16[128,2048]{1,0:T(8,128)(2,1)S(1)} %copy-done.45), channel_id=1, source_target_pairs={{0,2},{1,3},{2,0},{3,1},{4,6},{5,7},{6,4},{7,5},{8,10},{9,11},{10,... | collective-permute-start | bytes 1572872 | tf_op jit(solution)/shard_map/ppermute | solution.py:45
  458.6 56.7 %collective-permute-start.83 = (bf16[768,512]{1,0:T(8,128)(2,1)}, bf16[768,512]{1,0:T(8,128)(2,1)S(1)}, u32[]{:S(2)}, u32[]{:S(2)}) collective-permute-start(bf16[768,512]{1,0:T(8,128)(2,1)} %get-tuple-element.248), channel_id=1, source_target_pairs={{0,4},{4,0},{1,5},{5,1},{2,6},{6,2},{3,7},{7,3},{8,12},{12,8},{9,1... | collective-permute-start | bytes 2359304 | tf_op jit(solution)/shard_map/ppermute | solution.py:45
  489.2 68.0 %collective-permute-start.78 = (bf16[768,512]{1,0:T(8,128)(2,1)S(1)}, bf16[768,512]{1,0:T(8,128)(2,1)}, u32[]{:S(2)}, u32[]{:S(2)}) collective-permute-start(bf16[768,512]{1,0:T(8,128)(2,1)S(1)} %add_convert_fusion.2), channel_id=1, source_target_pairs={{0,16},{8,24},{16,0},{24,8},{1,17},{9,25},{17,1},{25,9},{2,18},{10... | collective-permute-start | bytes 2359304 | tf_op jit(solution)/shard_map/ppermute | solution.py:50
  491.7 68.2 %collective-permute-start.75 = (bf16[768,512]{1,0:T(8,128)(2,1)S(1)}, bf16[768,512]{1,0:T(8,128)(2,1)S(1)}, u32[]{:S(2)}, u32[]{:S(2)}) collective-permute-start(bf16[768,512]{1,0:T(8,128)(2,1)S(1)} %add_convert_fusion.3), channel_id=1, source_target_pairs={{0,8},{8,16},{16,24},{24,0},{1,9},{9,17},{17,25},{25,1},{2,10},{10... | collective-permute-start | bytes 2359304 | tf_op jit(solution)/shard_map/ppermute | solution.py:50
  517.2 42.7 %collective-permute-start.84 = (bf16[768,512]{1,0:T(8,128)(2,1)S(1)}, bf16[768,512]{1,0:T(8,128)(2,1)S(1)}, u32[]{:S(2)}, u32[]{:S(2)}) collective-permute-start(bf16[768,512]{1,0:T(8,128)(2,1)S(1)} %add_convert_fusion.refs_1_), channel_id=1, source_target_pairs={{0,4},{4,0},{1,5},{5,1},{2,6},{6,2},{3,7},{7,3},{8,12},{12,8},{9,1... | collective-permute-start | bytes 2359304 | tf_op jit(solution)/shard_map/ppermute | solution.py:45
  524.9 39.4 %collective-permute-start.82 = (bf16[768,512]{1,0:T(8,128)(2,1)S(1)}, bf16[768,512]{1,0:T(8,128)(2,1)S(1)}, u32[]{:S(2)}, u32[]{:S(2)}) collective-permute-start(bf16[768,512]{1,0:T(8,128)(2,1)S(1)} %collective-permute-done.81.refs_1_), channel_id=1, source_target_pairs={{0,4},{4,0},{1,5},{5,1},{2,6},{6,2},{3,7},{7,3},{8,12},{12,8},{9,1... | collective-permute-start | bytes 2359304 | tf_op jit(solution)/shard_map/ppermute | solution.py:45
  559.8 56.6 %collective-permute-start.71 = (bf16[2,512,512]{2,1,0:T(8,128)(2,1)}, bf16[2,512,512]{2,1,0:T(8,128)(2,1)}, u32[]{:S(2)}, u32[]{:S(2)}) collective-permute-start(bf16[2,512,512]{2,1,0:T(8,128)(2,1)} %pad_maximum_fusion.1), channel_id=1, source_target_pairs={{0,8},{8,0},{16,24},{24,16},{1,9},{9,1},{17,25},{25,17},{2,10},{10... | collective-permute-start | bytes 3145736 | tf_op jit(solution)/shard_map/ppermute | solution.py:45
  559.9 32.9 %collective-permute-start.66 = (bf16[512,384]{1,0:T(8,128)(2,1)}, bf16[512,384]{1,0:T(8,128)(2,1)}, u32[]{:S(2)}, u32[]{:S(2)}) collective-permute-start(bf16[512,384]{1,0:T(8,128)(2,1)} %get-tuple-element.222), channel_id=1, source_target_pairs={{0,4},{4,0},{1,5},{5,1},{2,6},{6,2},{3,7},{7,3},{8,12},{12,8},{9,1... | collective-permute-start | bytes 1179656 | tf_op jit(solution)/shard_map/ppermute | solution.py:45
  569.5 42.1 %collective-permute-start.76 = (bf16[768,512]{1,0:T(8,128)(2,1)S(1)}, bf16[768,512]{1,0:T(8,128)(2,1)}, u32[]{:S(2)}, u32[]{:S(2)}) collective-permute-start(bf16[768,512]{1,0:T(8,128)(2,1)S(1)} %collective-permute-done.75.refs_1_), channel_id=1, source_target_pairs={{0,4},{4,0},{1,5},{5,1},{2,6},{6,2},{3,7},{7,3},{8,12},{12,8},{9,1... | collective-permute-start | bytes 2359304 | tf_op jit(solution)/shard_map/ppermute | solution.py:45
  577.1 46.3 %collective-permute-start.56 = (bf16[256,2048]{1,0:T(8,128)(2,1)}, bf16[256,2048]{1,0:T(8,128)(2,1)S(1)}, u32[]{:S(2)}, u32[]{:S(2)}) collective-permute-start(bf16[256,2048]{1,0:T(8,128)(2,1)} %get-tuple-element.213), channel_id=1, source_target_pairs={{0,1},{1,0},{2,3},{3,2},{4,5},{5,4},{6,7},{7,6},{8,9},{9,8},{10,11... | collective-permute-start | bytes 3145736 | tf_op jit(solution)/shard_map/ppermute | solution.py:45
  592.8 64.7 %collective-permute-start.52 = (bf16[4,128,2048]{2,1,0:T(8,128)(2,1)}, bf16[4,128,2048]{2,1,0:T(8,128)(2,1)S(1)}, u32[]{:S(2)}, u32[]{:S(2)}) collective-permute-start(bf16[4,128,2048]{2,1,0:T(8,128)(2,1)} %get-tuple-element.207), channel_id=1, source_target_pairs={{0,2},{1,3},{2,0},{3,1},{4,6},{5,7},{6,4},{7,5},{8,10},{9,11},{10,... | collective-permute-start | bytes 6291464 | tf_op jit(solution)/shard_map/ppermute | solution.py:45
  611.7 59.0 %collective-permute-start.64 = (bf16[512,384]{1,0:T(8,128)(2,1)}, bf16[512,384]{1,0:T(8,128)(2,1)S(1)}, u32[]{:S(2)}, u32[]{:S(2)}) collective-permute-start(bf16[512,384]{1,0:T(8,128)(2,1)} %get-tuple-element.218), channel_id=1, source_target_pairs={{0,4},{4,0},{1,5},{5,1},{2,6},{6,2},{3,7},{7,3},{8,12},{12,8},{9,1... | collective-permute-start | bytes 1179656 | tf_op jit(solution)/shard_map/ppermute | solution.py:45
  (118 other events, 2281.8 us)
